TPU v7x, 512 devices: a whole 4x8x8 slice. The times are simulated.
512 devices in a mesh: req: 32 (over z, y_lo), tp: 16 (over y_hi, x, core).
Axes of the slice: x: 4, y: 8 (y_hi: 2, y_lo: 4; y = y_hi * 4 + y_lo), z: 8, core: 2. Of those that a mesh axis runs over, the one named last changes fastest.
Arguments:
- tokens: bfloat16 [16384, 4096], P(('req', 'tp')), parts along dimension 0, may hold values from -400 to 400
- norm_gain: bfloat16 [4096], replicated, may hold values from 0.099609375 to 1.8984375
- qkv_weight: bfloat16 [4096, 6144], P(None, 'tp'), may hold values from -0.46875 to 0.46875
- out_weight: bfloat16 [2048, 4096], P('tp'), may hold values from -0.5 to 0.5
- segment_ids: int32 [16384], P('req'), parts along dimension 0, may hold values from 0 to 7, never falling along the last dimension, each value on 1 to 170 neighbouring positions
- prefix_pages: int32 [256], P('req'), parts along dimension 0, may hold values from 1 to 16, 48 in all
- page_order: int32 [1536], P('req'), parts along dimension 0, may hold values from 0 to 47, each once
- fresh_order: int32 [1280], P('req'), parts along dimension 0, may hold values from 0 to 39, each once
- cache_pool: bfloat16 [2, 16, 1536, 16, 128], P(None, 'tp', 'req'), parts along dimension 2, may hold values from -6 to 6
Outputs:
- attn_out: bfloat16 [16384, 4096], P(('req', 'tp')), parts along dimension 0
- fresh_pages: bfloat16 [2, 16, 1280, 16, 128], P(None, 'tp', 'req'), parts along dimension 2
There are 32 independent parts, one for each index of `req`. A program takes and returns all parts, laid end to end along the dimension named above; an argument that names none is the same for every part. Nothing has to cross between parts.
Inputs may be any that keep to these rules, and one draw needn't show every extreme that they name: `segment_ids`: segment numbers never fall; every prompt has at least one new token and one has exactly 170. `prefix_pages`: they sum to 48; the largest is 16. `page_order`: every page once. `fresh_order`: every page once.
All inputs are finite; a program needn't handle non-finite values.
Results may differ from a plain program's by a relative error of at most 0.014.
Values may be sent and summed in bfloat16 or wider, within the bound.
No kernel may reach another device: no remote copies, remote signals or barrier semaphores. Data moves between devices by JAX's collectives and lax.ppermute only.
A program may use at most 64 MiB of HBM per device.

v0:
```python
import jax
import jax.numpy as jnp
from jax import lax
from jax.sharding import PartitionSpec as P

MODEL_HEADS = 32


def layer_norm(values, gain):
    values = values.astype(jnp.float32)
    center = values - jnp.mean(values, axis=-1, keepdims=True)
    spread = jnp.mean(center * center, axis=-1, keepdims=True)
    return (center * lax.rsqrt(spread + 1e-05) * gain.astype(jnp.float32)).astype(jnp.bfloat16)


def token_layout(segment_ids, prefix_pages, page_order, fresh_order, page_len):
    seq_count = prefix_pages.shape[0]
    tok_count = segment_ids.shape[0]
    labels = jnp.arange(seq_count, dtype=jnp.int32)
    member = (segment_ids[:, None] == labels[None, :]).astype(jnp.int32)
    counts = jnp.sum(member, axis=0)
    starts = jnp.cumsum(counts) - counts
    token_index = jnp.arange(tok_count, dtype=jnp.int32)
    in_prompt = token_index - jnp.sum(member * starts[None, :], axis=1)
    prefix_len = prefix_pages * page_len
    position = in_prompt + jnp.sum(member * prefix_len[None, :], axis=1)
    fresh_counts = (counts + page_len - 1) // page_len
    fresh_starts = jnp.cumsum(fresh_counts) - fresh_counts
    page_slot = jnp.sum(member * fresh_starts[None, :], axis=1) + in_prompt // page_len
    target = jnp.take(fresh_order, page_slot) * page_len + in_prompt % page_len
    page_count = page_order.shape[0]
    cache_starts = jnp.cumsum(prefix_pages) - prefix_pages
    logical = (
        jnp.zeros((page_count,), jnp.int32)
        .at[page_order]
        .set(jnp.arange(page_count, dtype=jnp.int32))
    )
    holder = jnp.sum((logical[:, None] >= cache_starts[None, :]).astype(jnp.int32), axis=1) - 1
    holder_start = jnp.sum(
        (holder[:, None] == labels[None, :]).astype(jnp.int32) * cache_starts[None, :], axis=1
    )
    slot_index = jnp.arange(page_len, dtype=jnp.int32)
    key_owner = jnp.repeat(holder, page_len)
    key_pos = ((logical - holder_start)[:, None] * page_len + slot_index[None, :]).reshape(-1)
    return (in_prompt, position, target, key_owner, key_pos)


def attention_mask(segment_ids, in_prompt, position, key_owner, key_pos):
    cache_ok = segment_ids[:, None] == key_owner[None, :]
    new_ok = (segment_ids[:, None] == segment_ids[None, :]) & (
        in_prompt[None, :] <= in_prompt[:, None]
    )
    allowed = jnp.concatenate([cache_ok, new_ok], axis=1)
    key_all = jnp.concatenate([key_pos, position])
    distance = (position[:, None] - key_all[None, :]).astype(jnp.float32)
    return (allowed, distance)


def attend_head(queries, key_rows, values, alibi_slope, allowed, distance):
    scores = lax.dot_general(
        queries, key_rows, (((1,), (1,)), ((), ())), preferred_element_type=jnp.float32
    )
    scores = scores * queries.shape[1] ** (-0.5) - alibi_slope * distance
    scores = jnp.where(allowed, scores, -1e30)
    peak_score = jnp.max(scores, axis=1, keepdims=True)
    weights = jnp.exp(scores - peak_score)
    weights_bf = (weights / jnp.sum(weights, axis=1, keepdims=True)).astype(jnp.bfloat16)
    return jnp.dot(weights_bf, values, preferred_element_type=jnp.float32).astype(jnp.bfloat16)


def body(
    tokens,
    norm_gain,
    qkv_weight,
    out_weight,
    segment_ids,
    prefix_pages,
    page_order,
    fresh_order,
    cache_pool,
):
    head_dev = cache_pool.shape[1]
    page_len = cache_pool.shape[3]
    head_size = cache_pool.shape[4]
    tp_size = lax.axis_size("tp")
    first_head = lax.axis_index("tp") * head_dev
    normed = layer_norm(tokens, norm_gain)
    projected = jnp.dot(
        lax.all_gather(normed, "tp", axis=0, tiled=True),
        qkv_weight,
        preferred_element_type=jnp.float32,
    ).astype(jnp.bfloat16)
    tok_count = projected.shape[0]
    in_prompt, position, target, key_owner, key_pos = token_layout(
        segment_ids, prefix_pages, page_order, fresh_order, page_len
    )
    allowed, distance = attention_mask(segment_ids, in_prompt, position, key_owner, key_pos)
    per_head = projected.reshape(tok_count, head_dev, 3, head_size)
    step_heads = MODEL_HEADS // (head_dev * tp_size)
    alibi_slope = jnp.exp2(
        -8.0 * (first_head + 0 + 1).astype(jnp.float32) * step_heads / MODEL_HEADS
    )
    key_rows = jnp.concatenate([cache_pool[0, 0].reshape(-1, head_size), per_head[:, 0, 1]], axis=0)
    values = jnp.concatenate([cache_pool[1, 0].reshape(-1, head_size), per_head[:, 0, 2]], axis=0)
    contexts = attend_head(per_head[:, 0, 0], key_rows, values, alibi_slope, allowed, distance)
    summed = lax.psum_scatter(
        jnp.dot(contexts, out_weight, preferred_element_type=jnp.float32).astype(jnp.bfloat16),
        "tp",
        scatter_dimension=0,
        tiled=True,
    )
    fresh_total = fresh_order.shape[0]
    new_kv = per_head[:, :, 1:3].transpose(2, 1, 0, 3)
    fresh_pages = (
        jnp.zeros((2, head_dev, fresh_total * page_len, head_size), jnp.bfloat16)
        .at[:, :, target]
        .set(new_kv)
    )
    return (summed, fresh_pages.reshape(2, head_dev, fresh_total, page_len, head_size))


def solution(mesh):
    placed = (
        P(("req", "tp"), None),
        P(),
        P(None, "tp"),
        P("tp", None),
        P("req"),
        P("req"),
        P("req"),
        P("req"),
        P(None, "tp", "req", None, None),
    )
    return jax.shard_map(
        body,
        mesh=mesh,
        in_specs=placed,
        out_specs=(P(("req", "tp"), None), P(None, "tp", "req", None, None)),
        check_vma=False,
    )
```

profile of v0, /device:TPU:8, one launch (start us, length us, event | category | flops | bytes accessed | tf_op | source)
XLA Modules:
  0.0 233.2 jit_solution(15736835718099933660)
XLA Ops:
  7.2 1.2 convert_reduce_fusion
  8.5 1.2 fusion.7
  10.4 1.8 fusion.9
  12.3 0.8 convert_reduce_fusion.1
  13.5 0.8 reduce-window.25
  16.9 0.8 select_reduce_fusion
  17.7 1.7 compare_and_fusion
  19.4 1.7 broadcast_compare_fusion
  21.1 1.8 fusion.26
  22.9 75.8 %all-gather.2.cloned.1.call-done = bf16[512,4096]{1,0:T(8,128)(2,1)} async-done(((bf16[32,4096]{1,0:T(8,128)(2,1)}), bf16[512,4096]{1,0:T(8,128)(2,1)}) %all-gather.2.cloned.1.call-update) | async-done | bytes 4194320 | tf_op jit(solution)/shard_map/all_gather | solution.py:89
  98.8 4.0 %convolution_convert_fusion.1 = bf16[512,384]{0,1:T(8,128)(2,1)S(1)} fusion(bf16[512,4096]{1,0:T(8,128)(2,1)} %all-gather.2.cloned.1.call-done, bf16[4096,384]{1,0:T(8,128)(2,1)S(1)} %copy-done), kind=kOutput, calls=%fused_computation.10 | convolution fusion | flops 1610809344 | bytes 7733248 | tf_op jit(solution)/shard_map/dot_general | solution.py:88
  102.8 0.8 slice_bitcast_fusion
  103.6 1.7 copy.20
  105.3 1.7 copy.19
  106.9 2.3 %fusion.30 = (f32[512]{0:T(512)S(1)}, f32[512,1280]{1,0:T(8,128)S(1)}) fusion(s32[1280]{0:T(1024)S(1)} %pad_add_fusion, s32[512]{0:T(512)} %copy-done.6, f32[]{:T(128)S(6)} %exp2.7, bf16[512,128]{1,0:T(8,128)(2,1)} %copy.19, bf16[768,128]{1,0:T(8,128)(2,1)} %bitcast.83, bf16[512,1,3,128]{0,3,2,1:T(8,128)(2,1)S(1)} %bitcast.80, ...), kind=kOutput, calls=%fused_computation.117 | convolution fusion | flops 173669888 | bytes 3747844 | tf_op jit(solution)/shard_map/dot_general | solution.py:60
  109.3 1.5 copy-done.1
  111.3 6.3 %convolution_convert_fusion = bf16[512,4096]{1,0:T(8,128)(2,1)} fusion(bf16[128,4096]{1,0:T(8,128)(2,1)} %param.12, f32[512,1280]{1,0:T(8,128)} %copy-done.1, f32[512]{0:T(512)S(1)} %fusion.2, f32[512]{0:T(512)} %copy-done.7, bf16[512,128]{1,0:T(8,128)(2,1)S(1)} %copy-done.5, bf16[768,128]{1,0:T(8,128)(2,1)S(1)} %bitcast.82), kind=kOutput, calls=%fused_computation.2 | convolution fusion | flops 709427200 | bytes 8196096 | tf_op jit(solution)/shard_map/dot_general | solution.py:107
  120.4 4.5 %compare_select_fusion.2 = (s32[512,1]{0,1:T(1,128)S(1)}, s32[512,1]{0,1:T(1,128)S(1)}) fusion(s32[]{:T(128)} %bitcast.46, s32[]{:T(128)} %bitcast.47, s32[]{:T(128)} %bitcast.48, s32[]{:T(128)} %bitcast.49, s32[]{:T(128)} %bitcast.50, s32[]{:T(128)} %bitcast.52, s32[]{:T(128)} %bitcast.51, s32[512,1]{0,1:T(1,128)S(1)} %bitcast.87, s32[512,1]{0,1:T(1,128)S(1)} %bitcast.84), kind=kLoop, calls=%fused_computation.72 | loop fusion | flops 16384 | bytes 8220 | tf_op jit(solution)/shard_map/jit(_take)/gather | solution.py:30
  125.1 20.5 %select_select_fusion = s32[512]{0:T(512)S(1)} fusion(pred[512]{0:T(512)(128)(4,1)S(1)} %get-tuple-element.39, pred[512]{0:T(512)(128)(4,1)S(1)} %get-tuple-element.38, pred[512]{0:T(512)(128)(4,1)S(1)} %get-tuple-element.40, pred[512]{0:T(512)(128)(4,1)S(1)} %get-tuple-element.37, pred[512]{0:T(512)(128)(4,1)S(1)} %get-tuple-element.36, ...), kind=kLoop, calls=%fused_computation.89 | loop fusion | flops 16896 | bytes 21124 | tf_op jit(solution)/shard_map/jit(_take)/gather | solution.py:30
  145.7 1.0 slice.68
  146.7 0.9 copy.23
  147.7 29.9 %scatter_fusion = bf16[2,640,128]{2,0,1:T(2,128)(2,1)S(1)} fusion(bf16[2,640,128]{2,0,1:T(2,128)(2,1)S(1)} %broadcast.454, s32[512]{0:T(512)S(1)} %bitcast.86, bf16[512,2,128]{2,1,0:T(2,128)(2,1)} %bitcast.78), kind=kCustom, calls=%fused_computation.1 | custom fusion | bytes 788480 | tf_op jit(solution)/shard_map/scatter | solution.py:117
  177.6 0.8 copy.22
  178.3 48.1 %reduce-scatter.2.cloned.1.call-done = bf16[32,4096]{1,0:T(8,128)(2,1)} async-done(((bf16[512,4096]{1,0:T(8,128)(2,1)}), bf16[32,4096]{1,0:T(8,128)(2,1)}) %reduce-scatter.2.cloned.1.call-update) | async-done | bytes 262160 | tf_op jit(solution)/shard_map/reduce_scatter | solution.py:106
  (46 shorter events, 7.5 us)
Async XLA Ops:
  7.2 91.6 %copy-start = (bf16[4096,384]{1,0:T(8,128)(2,1)S(1)}, bf16[4096,384]{1,0:T(8,128)(2,1)}, u32[]{:S(2)}) copy-start(bf16[4096,384]{1,0:T(8,128)(2,1)} %param.11) | copy-start | bytes 9437188
  7.2 91.6 %all-gather.2.cloned.1.call-start = ((), (), s32[]{:S(2)}) async-start(), calls=%async_computation.1 | async-start | bytes 4456448 | tf_op jit(solution)/shard_map/all_gather | solution.py:89
  12.2 214.2 %reduce-scatter.2.cloned.1.call-start = ((), (), s32[]{:S(2)}) async-start(), calls=%async_computation.2 | async-start | bytes 4456448 | tf_op jit(solution)/shard_map/reduce_scatter | solution.py:106
  17.7 5.3 %copy-start.6 = (s32[512]{0:T(512)}, s32[512]{0:T(512)S(1)}, u32[]{:S(2)}) copy-start(s32[512]{0:T(512)S(1)} %get-tuple-element.50) | copy-start | bytes 6148
  102.8 6.4 %copy-start.3 = (bf16[512,384]{0,1:T(8,128)(2,1)}, bf16[512,384]{0,1:T(8,128)(2,1)S(1)}, u32[]{:S(2)}) copy-start(bf16[512,384]{0,1:T(8,128)(2,1)S(1)} %convolution_convert_fusion.1) | copy-start | bytes 1179652
  109.3 1.5 copy-start.1
  109.3 2.0 copy-start.7
  109.3 2.0 copy-start.4
  109.3 2.0 copy-start.5
  117.7 0.7 copy-start.2
Sparse Core Ops, SparseCore 0:
  12.3 86.4 all-gather.1
  117.8 108.5 reduce-scatter.1
where the time goes:
time: 236 us; the launch traced here: 233 us
  waiting for transfers between devices  124 us (53%)
  local copies, waits for them, and re-layouts  43.7 us (19%)
  other arithmetic  38.6 us (16%)
  between operations  14.3 us (6%)
  matrix products  12.7 us (5%)
    all_gather x1, waiting for transfers between devices, body(): lax.all_gather(normed, 'tp', axis=0, tiled=True)  75.8 us
    reduce_scatter x1, waiting for transfers between devices, body(): lax.psum_scatter(jnp.dot(contexts, out_weight, preferred_element_type=jnp...  48.1 us
    scatter x1, local copies, waits for them, and re-layouts, body(): fresh_pages = jnp.zeros((2, head_dev, fresh_total * page_len, head_size),...  29.9 us
    gather x3, other arithmetic, token_layout(): target = jnp.take(fresh_order, page_slot) * page_len + in_prompt % page_len  25.2 us
    dot_general x1, matrix products, body(): jnp.dot(contexts, out_weight, preferred_element_type=jnp.float32)  6.32 us
  transfers between devices with their start and end apart: 2, of which 2 were waited for; matrix products, arithmetic and copies ran while one was open for 30% of the time, Pallas kernels for 0%

commit v1 on v0

v1 whole, which is shorter than its diff:
```python
import jax
import jax.numpy as jnp
from jax import lax
from jax.experimental import pallas as pl
from jax.experimental.pallas import tpu as pltpu
from jax.sharding import PartitionSpec as P


MODEL_HEADS = 32
N_X = 4
N_TP = 16
BLOCK = 32
PAGE = 16
SEQS = 8
HEAD = 128
FAR = 3e32


def tp_of(y, x, c):
    return (y % 2) * 8 + (x % N_X) * 2 + c % 2


def moved(value, dy, dx, dc):
    pairs = [
        (tp_of(y, x, c), tp_of(y + dy, x + dx, c + dc))
        for y in range(2)
        for x in range(N_X)
        for c in range(2)
    ]
    return lax.ppermute(value, "tp", pairs)


def my_place():
    me = lax.axis_index("tp")
    return me >> 3, (me >> 1) & 3, me & 1


def layout_kernel(seg_ref, prefix_ref, order_ref, fresh_ref, dist_ref, target_ref):
    y, x, c = my_place()
    seg = seg_ref[...]
    starts = [jnp.int32(0)]
    for s in range(1, SEQS):
        starts.append(jnp.sum((seg < s).astype(jnp.float32)).astype(jnp.int32))
    ends = starts[1:] + [jnp.int32(seg.shape[0] * seg.shape[1])]
    cache_starts = [jnp.int32(0)]
    fresh_starts = [jnp.int32(0)]
    for s in range(SEQS):
        cache_starts.append(cache_starts[s] + prefix_ref[s])
        fresh_starts.append(fresh_starts[s] + ((ends[s] - starts[s] + PAGE - 1) >> 4))

    def pick(token, values):
        result = jnp.full(token.shape, values[0], jnp.int32)
        for s in range(1, SEQS):
            result = jnp.where(token >= starts[s], values[s], result)
        return result

    row = lax.broadcasted_iota(jnp.int32, (8, 128), 0)
    lane = lax.broadcasted_iota(jnp.int32, (8, 128), 1)
    physical = row * 128 + lane
    page = physical >> 4
    slot = jnp.zeros((8, 128), jnp.int32)
    for i in range(order_ref.shape[0]):
        slot = jnp.where(page == order_ref[i], i * PAGE, slot)
    slot = slot + (physical & (PAGE - 1))
    slot_owner = jnp.zeros((8, 128), jnp.int32)
    for s in range(1, SEQS):
        slot_owner = slot_owner + (slot >= cache_starts[s] * PAGE).astype(jnp.int32)

    yy, cc, dx = row & 1, row >> 1, lane >> 5
    holder = ((y + yy) & 1) * 8 + ((x - dx) & 3) * 2 + ((c + cc) & 1)
    token = holder * BLOCK + (lane & (BLOCK - 1))
    token_owner = pick(token, list(range(SEQS)))
    in_prompt = token - pick(token, starts)
    page_slot = pick(token, fresh_starts[:SEQS]) + (in_prompt >> 4)
    fresh_page = jnp.zeros((8, 128), jnp.int32)
    for i in range(fresh_ref.shape[0]):
        fresh_page = jnp.where(page_slot == i, fresh_ref[i], fresh_page)
    target_ref[...] = fresh_page * PAGE + (in_prompt & (PAGE - 1))

    base = [cache_starts[s + 1] * PAGE - starts[s] for s in range(SEQS)]
    for b in range(8):
        at = ((y + b // 4) & 1) * 8 + ((x - b % 4) & 3) * 2 + c
        query = at * BLOCK + lax.broadcasted_iota(jnp.int32, (BLOCK, 128), 0)
        owner = pick(query, list(range(SEQS)))
        reach = pick(query, base) + query
        rows = slice(b * BLOCK, (b + 1) * BLOCK)
        for k in range(6):
            apart = (reach - slot[k : k + 1, :]).astype(jnp.float32)
            dist_ref[rows, k * 128 : (k + 1) * 128] = jnp.where(
                owner == slot_owner[k : k + 1, :], apart, FAR
            )
        for k in range(4):
            gap = query - token[k : k + 1, :]
            usable = (owner == token_owner[k : k + 1, :]) & (gap >= 0)
            dist_ref[rows, (6 + k) * 128 : (7 + k) * 128] = jnp.where(
                usable, gap.astype(jnp.float32), FAR
            )


def layout_tables(segment_ids, prefix_pages, page_order, fresh_order):
    smem = pl.BlockSpec(memory_space=pltpu.SMEM)
    vmem = pl.BlockSpec(memory_space=pltpu.VMEM)
    return pl.pallas_call(
        layout_kernel,
        out_shape=(
            jax.ShapeDtypeStruct((256, 1280), jnp.float32),
            jax.ShapeDtypeStruct((8, 128), jnp.int32),
        ),
        in_specs=[vmem, smem, smem, smem],
        out_specs=(vmem, vmem),
        cost_estimate=pl.CostEstimate(flops=0, bytes_accessed=4_000_000, transcendentals=0),
        name="layout",
    )(segment_ids.reshape(4, 128), prefix_pages, page_order, fresh_order)


def project_kernel(a_ref, b_ref, c_ref, d_ref, gain_ref, mine_ref, other_ref, q_ref, kv_ref, normed, total):
    step = pl.program_id(0)
    depth = mine_ref.shape[0]

    @pl.when(step == 0)
    def _():
        gain = gain_ref[...].astype(jnp.float32)
        for i, ref in enumerate((a_ref, b_ref, c_ref, d_ref)):
            for h in range(2):
                rows = slice(h * 16, (h + 1) * 16)
                values = ref[rows, :].astype(jnp.float32)
                center = values - jnp.mean(values, axis=-1, keepdims=True)
                spread = jnp.mean(center * center, axis=-1, keepdims=True)
                result = (center * lax.rsqrt(spread + 1e-05) * gain).astype(jnp.bfloat16)
                for k in range(normed.shape[0]):
                    normed[k, i * BLOCK + h * 16 : i * BLOCK + (h + 1) * 16, :] = result[
                        :, k * depth : (k + 1) * depth
                    ]
        total[...] = jnp.zeros_like(total)

    left = normed[step]
    total[:, :384] += jnp.dot(left, mine_ref[...], preferred_element_type=jnp.float32)
    total[:, 384:] += jnp.dot(left, other_ref[...], preferred_element_type=jnp.float32)

    @pl.when(step == pl.num_programs(0) - 1)
    def _():
        done = total[...].astype(jnp.bfloat16)
        q_ref[:, :128] = done[:, :128]
        q_ref[:, 128:] = done[:, 384:512]
        kv_ref[:, :256] = done[:, 128:384]
        kv_ref[:, 256:] = done[:, 512:]


def project(pieces, gain, mine, other):
    steps = 4
    depth = mine.shape[0] // steps
    whole = lambda shape: pl.BlockSpec(shape, lambda k: (0, 0))
    return pl.pallas_call(
        project_kernel,
        grid=(steps,),
        out_shape=(
            jax.ShapeDtypeStruct((128, 256), jnp.bfloat16),
            jax.ShapeDtypeStruct((128, 512), jnp.bfloat16),
        ),
        in_specs=[whole((BLOCK, 4096))] * 4
        + [whole((1, 4096))]
        + [pl.BlockSpec((depth, 384), lambda k: (k, 0))] * 2,
        out_specs=(whole((128, 256)), whole((128, 512))),
        scratch_shapes=[
            pltpu.VMEM((steps, 128, depth), jnp.bfloat16),
            pltpu.VMEM((128, 768), jnp.float32),
        ],
        compiler_params=pltpu.CompilerParams(dimension_semantics=("arbitrary",)),
        cost_estimate=pl.CostEstimate(
            flops=2 * 128 * 4096 * 768, bytes_accessed=7_500_000, transcendentals=0
        ),
        name="project",
    )(*pieces, gain.reshape(1, 4096), mine, other)


def attend_kernel(
    qa_ref, qb_ref, kva_ref, kvb_ref, kvc_ref, kvd_ref, mine_ref, other_ref, dist_ref,
    out_mine_ref, out_other_ref, *rest,
):
    out_refs, (scores, weights, queries, context) = rest[:8], rest[8:]
    y, x, c = my_place()
    cached = (mine_ref, other_ref)
    for head in range(2):
        columns = slice(head * HEAD, (head + 1) * HEAD)
        at = (y * 8 + x * 2 + (c ^ head) + 1).astype(jnp.float32)
        slope = jnp.exp2(jnp.full((1, 128), -8.0 * (MODEL_HEADS // N_TP) / MODEL_HEADS, jnp.float32) * at)
        queries[:128, :] = qa_ref[:, columns]
        queries[128:, :] = qb_ref[:, columns]
        q = queries[...]
        near, far = slice(head * 256, head * 256 + 128), slice(head * 256 + 128, head * 256 + 256)
        away = slice((1 - head) * 256, (1 - head) * 256 + 128)
        away_v = slice((1 - head) * 256 + 128, (1 - head) * 256 + 256)
        new = ((kva_ref, near, far), (kvb_ref, near, far), (kvc_ref, away, away_v), (kvd_ref, away, away_v))
        turned = (((1,), (1,)), ((), ()))
        scores[:, :768] = lax.dot_general(
            q, cached[head][0, 0].reshape(768, HEAD), turned, preferred_element_type=jnp.float32
        )
        for i, (ref, keys, _) in enumerate(new):
            scores[:, 768 + i * 128 : 896 + i * 128] = lax.dot_general(
                q, ref[:, keys], turned, preferred_element_type=jnp.float32
            )
        sums = []
        for b in range(8):
            rows = slice(b * BLOCK, (b + 1) * BLOCK)
            pieces = []
            peak = None
            for k in range(10):
                lanes = slice(k * 128, (k + 1) * 128)
                piece = scores[rows, lanes] * HEAD ** (-0.5) - slope * dist_ref[rows, lanes]
                peak = piece if peak is None else jnp.maximum(peak, piece)
                pieces.append(piece)
            peak = jnp.max(peak, axis=1, keepdims=True)
            total = None
            for k in range(10):
                weight = jnp.exp(pieces[k] - peak)
                total = weight if total is None else total + weight
                weights[rows, k * 128 : (k + 1) * 128] = weight.astype(jnp.bfloat16)
            sums.append(jnp.sum(total, axis=1, keepdims=True))
        result = jnp.dot(
            weights[:, :768], cached[head][1, 0].reshape(768, HEAD), preferred_element_type=jnp.float32
        )
        for i, (ref, _, values) in enumerate(new):
            result = result + jnp.dot(
                weights[:, 768 + i * 128 : 896 + i * 128], ref[:, values], preferred_element_type=jnp.float32
            )
        for b in range(8):
            context[b * BLOCK : (b + 1) * BLOCK, columns] = (
                result[b * BLOCK : (b + 1) * BLOCK] / sums[b]
            ).astype(jnp.bfloat16)
    left, right = context[:, :HEAD], context[:, HEAD:]
    for n in range(8):
        lanes = slice(n * 512, (n + 1) * 512)
        partial = (
            jnp.dot(left, out_mine_ref[:, lanes], preferred_element_type=jnp.float32)
            + jnp.dot(right, out_other_ref[:, lanes], preferred_element_type=jnp.float32)
        ).astype(jnp.bfloat16)
        for b in range(8):
            out_refs[b][:, lanes] = partial[b * BLOCK : (b + 1) * BLOCK]


def attend(queries, pairs, mine, other, dist, out_mine, out_other):
    vmem = pl.BlockSpec(memory_space=pltpu.VMEM)
    return pl.pallas_call(
        attend_kernel,
        out_shape=[jax.ShapeDtypeStruct((BLOCK, 4096), jnp.bfloat16)] * 8,
        in_specs=[vmem] * 11,
        out_specs=[vmem] * 8,
        scratch_shapes=[
            pltpu.VMEM((256, 1280), jnp.float32),
            pltpu.VMEM((256, 1280), jnp.bfloat16),
            pltpu.VMEM((256, HEAD), jnp.bfloat16),
            pltpu.VMEM((256, 256), jnp.bfloat16),
        ],
        cost_estimate=pl.CostEstimate(
            flops=4 * 256 * 1280 * 256 + 2 * 256 * 256 * 4096,
            bytes_accessed=7_000_000,
            transcendentals=2 * 256 * 1280,
        ),
        name="attend",
    )(*queries, *pairs, mine, other, dist, out_mine, out_other)


def fresh_kernel(target_ref, kva_ref, kvb_ref, kvc_ref, kvd_ref, out_ref):
    total = out_ref.shape[1]
    places = lax.broadcasted_iota(jnp.int32, (total, 128), 0)
    result = None
    for i, ref in enumerate((kva_ref, kvb_ref, kvc_ref, kvd_ref)):
        columns = slice(0, 256) if i < 2 else slice(256, 512)
        chosen = (places == target_ref[i : i + 1, :]).astype(jnp.float32).astype(jnp.bfloat16)
        part = jnp.dot(chosen, ref[:, columns], preferred_element_type=jnp.float32)
        result = part if result is None else result + part
    out_ref[0] = result[:, :HEAD].astype(jnp.bfloat16)
    out_ref[1] = result[:, HEAD:].astype(jnp.bfloat16)


def fresh(target, pairs, pages):
    vmem = pl.BlockSpec(memory_space=pltpu.VMEM)
    return pl.pallas_call(
        fresh_kernel,
        out_shape=jax.ShapeDtypeStruct((2, pages * PAGE, HEAD), jnp.bfloat16),
        in_specs=[vmem] * 5,
        out_specs=vmem,
        cost_estimate=pl.CostEstimate(
            flops=2 * 640 * 512 * 256, bytes_accessed=2_000_000, transcendentals=0
        ),
        name="fresh",
    )(target, *pairs)


def body(
    tokens,
    norm_gain,
    qkv_weight,
    out_weight,
    segment_ids,
    prefix_pages,
    page_order,
    fresh_order,
    cache_pool,
):
    partner = moved(tokens, 1, 0, 0)
    own = [tokens]
    for dx in (1, 2, 3):
        own.append(moved(tokens, 0, dx, 0))
    qkv_other = moved(qkv_weight, 0, 0, 1)
    out_other = moved(out_weight, 0, 0, 1)
    cache_other = moved(cache_pool, 0, 0, 1)
    across = [partner]
    for dx in (1, 2, 3):
        across.append(moved(partner, 0, dx, 0))
    dist, target = layout_tables(segment_ids, prefix_pages, page_order, fresh_order)
    q_own, kv_own = project(own, norm_gain, qkv_weight, qkv_other)
    kv_own_other = moved(kv_own, 0, 0, 1)
    q_across, kv_across = project(across, norm_gain, qkv_weight, qkv_other)
    kv_across_other = moved(kv_across, 0, 0, 1)
    pairs = (kv_own, kv_across, kv_own_other, kv_across_other)
    partial = attend((q_own, q_across), pairs, cache_pool, cache_other, dist, out_weight, out_other)
    kept, passed = partial[:4], partial[4:]
    passed_in, kept_in = [], []
    for dx in (2, 1, 3):
        passed_in.append(moved(passed[dx], 0, -dx, 0))
    for dx in (2, 1, 3):
        kept_in.append(moved(kept[dx], 0, -dx, 0))

    def added(first, others):
        total = first.astype(jnp.float32)
        for other in others:
            total = total + other.astype(jnp.float32)
        return total

    passed_sum = added(passed[0], passed_in).astype(jnp.bfloat16)
    from_partner = moved(passed_sum, 1, 0, 0)
    fresh_pages = fresh(target, pairs, fresh_order.shape[0])
    summed = added(kept[0], kept_in + [from_partner]).astype(jnp.bfloat16)
    return (summed, fresh_pages.reshape(2, 1, fresh_order.shape[0], PAGE, HEAD))


def solution(mesh):
    placed = (
        P(("req", "tp"), None),
        P(),
        P(None, "tp"),
        P("tp", None),
        P("req"),
        P("req"),
        P("req"),
        P("req"),
        P(None, "tp", "req", None, None),
    )
    return jax.shard_map(
        body,
        mesh=mesh,
        in_specs=placed,
        out_specs=(P(("req", "tp"), None), P(None, "tp", "req", None, None)),
        check_vma=False,
    )
```

time: 236 us -> 125 us (0.53)
  the two profiles are of different devices: /device:TPU:8 before, /device:TPU:32 now
where the time goes in v1:
time: 125 us
  starting transfers between devices  63.5 us (51%)
  waiting for transfers between devices  31.6 us (25%)
  Pallas kernels  23.5 us (19%)
  other arithmetic  2.91 us (2%)
  local copies, waits for them, and re-layouts  2.13 us (2%)
    ppermute x19, starting transfers between devices, moved(): return lax.ppermute(value, 'tp', pairs)  63.5 us
    ppermute x19, waiting for transfers between devices, moved(): return lax.ppermute(value, 'tp', pairs)  31.6 us
    pallas_call x2, Pallas kernels, project(): pl.pallas_call(project_kernel, grid=(steps,), out_shape=(jax.ShapeDtypeSt...  12.1 us
    pallas_call x1, Pallas kernels, attend(): pl.pallas_call(attend_kernel, out_shape=[jax.ShapeDtypeStruct((BLOCK, 409...  6.74 us
  transfers between devices with their start and end apart: 19, of which 4 were waited for; matrix products, arithmetic and copies ran while one was open for 2% of the time, Pallas kernels for 13%

profile of v1, /device:TPU:32, one launch (start us, length us, event | category | flops | bytes accessed | tf_op | source)
XLA Modules:
  0.0 124.5 jit_solution(1223850938809675317)
XLA Ops:
  2.6 2.4 %collective-permute-start.11 = (bf16[128,4096]{1,0:T(8,128)(2,1)}, bf16[128,4096]{1,0:T(8,128)(2,1)}, u32[]{:S(2)}, u32[]{:S(2)}) collective-permute-start(bf16[128,4096]{1,0:T(8,128)(2,1)} %out_mine_ref.1), channel_id=1, source_target_pairs={{0,1},{1,0},{2,3},{3,2},{4,5},{5,4},{6,7},{7,6},{8,9},{9,8},{10,11... | collective-permute-start | bytes 3145736 | tf_op jit(solution)/shard_map/ppermute | solution.py:30
  5.0 7.4 %collective-permute-start.4 = (bf16[32,4096]{1,0:T(8,128)(2,1)}, bf16[32,4096]{1,0:T(8,128)(2,1)S(1)}, u32[]{:S(2)}, u32[]{:S(2)}) collective-permute-start(bf16[32,4096]{1,0:T(8,128)(2,1)} %a_ref.1), channel_id=1, source_target_pairs={{0,8},{1,9},{2,10},{3,11},{4,12},{5,13},{6,14},{7,15},{8,0},{9,1},... | collective-permute-start | bytes 786440 | tf_op jit(solution)/shard_map/ppermute | solution.py:30
  12.3 12.3 %collective-permute-done.4.a_ref = bf16[32,4096]{1,0:T(8,128)(2,1)S(1)} collective-permute-done((bf16[32,4096]{1,0:T(8,128)(2,1)}, bf16[32,4096]{1,0:T(8,128)(2,1)S(1)}, u32[]{:S(2)}, u32[]{:S(2)}) %collective-permute-start.4) | collective-permute-done | bytes 262176 | tf_op jit(solution)/shard_map/ppermute | solution.py:30
  24.6 3.6 %collective-permute-start.5 = (bf16[32,4096]{1,0:T(8,128)(2,1)S(1)}, bf16[32,4096]{1,0:T(8,128)(2,1)S(1)}, u32[]{:S(2)}, u32[]{:S(2)}) collective-permute-start(bf16[32,4096]{1,0:T(8,128)(2,1)S(1)} %collective-permute-done.4.a_ref), channel_id=1, source_target_pairs={{0,2},{1,3},{2,4},{3,5},{4,6},{5,7},{6,0},{7,1},{8,10},{9,11},{10,... | collective-permute-start | bytes 786440 | tf_op jit(solution)/shard_map/ppermute | solution.py:30
  28.3 4.6 %collective-permute-start.6 = (bf16[32,4096]{1,0:T(8,128)(2,1)S(1)}, bf16[32,4096]{1,0:T(8,128)(2,1)S(1)}, u32[]{:S(2)}, u32[]{:S(2)}) collective-permute-start(bf16[32,4096]{1,0:T(8,128)(2,1)S(1)} %collective-permute-done.4.a_ref), channel_id=1, source_target_pairs={{0,4},{1,5},{2,6},{3,7},{4,0},{5,1},{6,2},{7,3},{8,12},{9,13},{10,... | collective-permute-start | bytes 786440 | tf_op jit(solution)/shard_map/ppermute | solution.py:30
  32.9 3.3 %collective-permute-start.7 = (bf16[32,4096]{1,0:T(8,128)(2,1)S(1)}, bf16[32,4096]{1,0:T(8,128)(2,1)S(1)}, u32[]{:S(2)}, u32[]{:S(2)}) collective-permute-start(bf16[32,4096]{1,0:T(8,128)(2,1)S(1)} %collective-permute-done.4.a_ref), channel_id=1, source_target_pairs={{0,6},{1,7},{2,0},{3,1},{4,2},{5,3},{6,4},{7,5},{8,14},{9,15},{10,... | collective-permute-start | bytes 786440 | tf_op jit(solution)/shard_map/ppermute | solution.py:30
  36.3 5.3 %collective-permute-done.5.b_ref = bf16[32,4096]{1,0:T(8,128)(2,1)S(1)} collective-permute-done((bf16[32,4096]{1,0:T(8,128)(2,1)S(1)}, bf16[32,4096]{1,0:T(8,128)(2,1)S(1)}, u32[]{:S(2)}, u32[]{:S(2)}) %collective-permute-start.5) | collective-permute-done | bytes 262176 | tf_op jit(solution)/shard_map/ppermute | solution.py:30
  43.5 2.9 %collective-permute-start.1 = (bf16[32,4096]{1,0:T(8,128)(2,1)}, bf16[32,4096]{1,0:T(8,128)(2,1)}, u32[]{:S(2)}, u32[]{:S(2)}) collective-permute-start(bf16[32,4096]{1,0:T(8,128)(2,1)} %a_ref.1), channel_id=1, source_target_pairs={{0,4},{1,5},{2,6},{3,7},{4,0},{5,1},{6,2},{7,3},{8,12},{9,13},{10,... | collective-permute-start | bytes 786440 | tf_op jit(solution)/shard_map/ppermute | solution.py:30
  46.5 4.1 %collective-permute-start.2 = (bf16[32,4096]{1,0:T(8,128)(2,1)}, bf16[32,4096]{1,0:T(8,128)(2,1)}, u32[]{:S(2)}, u32[]{:S(2)}) collective-permute-start(bf16[32,4096]{1,0:T(8,128)(2,1)} %a_ref.1), channel_id=1, source_target_pairs={{0,6},{1,7},{2,0},{3,1},{4,2},{5,3},{6,4},{7,5},{8,14},{9,15},{10,... | collective-permute-start | bytes 786440 | tf_op jit(solution)/shard_map/ppermute | solution.py:30
  53.9 6.0 %project.3 = (bf16[128,256]{1,0:T(8,128)(2,1)}, bf16[128,512]{1,0:T(8,128)(2,1)}) custom-call(bf16[32,4096]{1,0:T(8,128)(2,1)} %copy-done.4, bf16[32,4096]{1,0:T(8,128)(2,1)} %copy-done.5, bf16[32,4096]{1,0:T(8,128)(2,1)} %copy-done.6, bf16[32,4096]{1,0:T(8,128)(2,1)} %copy-done.7, bf16[1,4096]{1,0:T(2,128)(2,1)} %reshape.14.gain_ref, ...), custom_call_target="tpu_custom_call" | custom-call | flops 805306368 | bytes 7500000 | tf_op jit(solution)/shard_map/project/pallas_call | solution.py:153
  59.9 2.4 %collective-permute-start.9 = (bf16[128,512]{1,0:T(8,128)(2,1)}, bf16[128,512]{1,0:T(8,128)(2,1)S(1)}, u32[]{:S(2)}, u32[]{:S(2)}) collective-permute-start(bf16[128,512]{1,0:T(8,128)(2,1)} %get-tuple-element.19.kvb_ref), channel_id=1, source_target_pairs={{0,1},{1,0},{2,3},{3,2},{4,5},{5,4},{6,7},{7,6},{8,9},{9,8},{10,11... | collective-permute-start | bytes 393224 | tf_op jit(solution)/shard_map/ppermute | solution.py:30
  62.3 6.0 %project.2 = (bf16[128,256]{1,0:T(8,128)(2,1)}, bf16[128,512]{1,0:T(8,128)(2,1)}) custom-call(bf16[32,4096]{1,0:T(8,128)(2,1)} %a_ref.1, bf16[32,4096]{1,0:T(8,128)(2,1)} %collective-permute-done.b_ref, bf16[32,4096]{1,0:T(8,128)(2,1)} %collective-permute-done.1.c_ref, bf16[32,4096]{1,0:T(8,128)(2,1)} %collective-permute-done.2.d_ref, ...), custom_call_target="tpu_custom_call" | custom-call | flops 805306368 | bytes 7500000 | tf_op jit(solution)/shard_map/project/pallas_call | solution.py:153
  70.3 2.4 %layout.1 = (f32[256,1280]{1,0:T(8,128)}, s32[8,128]{1,0:T(8,128)}) custom-call(s32[4,128]{1,0:T(4,128)} %bitcast.5, s32[8]{0:T(128)} %prefix_ref.1, s32[48]{0:T(128)} %order_ref.1, s32[40]{0:T(128)} %fresh_ref.1), custom_call_target="tpu_custom_call" | custom-call | bytes 4000000 | tf_op jit(solution)/shard_map/layout/pallas_call | solution.py:103
  73.5 6.7 %attend.1 = (bf16[32,4096]{1,0:T(8,128)(2,1)}, bf16[32,4096]{1,0:T(8,128)(2,1)}, bf16[32,4096]{1,0:T(8,128)(2,1)}, bf16[32,4096]{1,0:T(8,128)(2,1)}, bf16[32,409...) custom-call(bf16[128,256]{1,0:T(8,128)(2,1)} %get-tuple-element.16.qa_ref, ...), custom_call_target="tpu_custom_call" | custom-call | flops 872415232 | bytes 7000000 | tf_op jit(solution)/shard_map/attend/pallas_call | solution.py:243
  80.2 4.8 %collective-permute-start.15 = (bf16[32,4096]{1,0:T(8,128)(2,1)}, bf16[32,4096]{1,0:T(8,128)(2,1)S(1)}, u32[]{:S(2)}, u32[]{:S(2)}) collective-permute-start(bf16[32,4096]{1,0:T(8,128)(2,1)} %get-tuple-element.26), channel_id=1, source_target_pairs={{0,4},{1,5},{2,6},{3,7},{4,0},{5,1},{6,2},{7,3},{8,12},{9,13},{10,... | collective-permute-start | bytes 786440 | tf_op jit(solution)/shard_map/ppermute | solution.py:30
  85.1 2.5 %collective-permute-start.16 = (bf16[32,4096]{1,0:T(8,128)(2,1)}, bf16[32,4096]{1,0:T(8,128)(2,1)S(1)}, u32[]{:S(2)}, u32[]{:S(2)}) collective-permute-start(bf16[32,4096]{1,0:T(8,128)(2,1)} %get-tuple-element.27), channel_id=1, source_target_pairs={{0,6},{1,7},{2,0},{3,1},{4,2},{5,3},{6,4},{7,5},{8,14},{9,15},{10,... | collective-permute-start | bytes 786440 | tf_op jit(solution)/shard_map/ppermute | solution.py:30
  87.6 3.3 %collective-permute-start.17 = (bf16[32,4096]{1,0:T(8,128)(2,1)}, bf16[32,4096]{1,0:T(8,128)(2,1)S(1)}, u32[]{:S(2)}, u32[]{:S(2)}) collective-permute-start(bf16[32,4096]{1,0:T(8,128)(2,1)} %get-tuple-element.28), channel_id=1, source_target_pairs={{0,2},{1,3},{2,4},{3,5},{4,6},{5,7},{6,0},{7,1},{8,10},{9,11},{10,... | collective-permute-start | bytes 786440 | tf_op jit(solution)/shard_map/ppermute | solution.py:30
  90.9 2.5 %collective-permute-start.12 = (bf16[32,4096]{1,0:T(8,128)(2,1)}, bf16[32,4096]{1,0:T(8,128)(2,1)S(1)}, u32[]{:S(2)}, u32[]{:S(2)}) collective-permute-start(bf16[32,4096]{1,0:T(8,128)(2,1)} %get-tuple-element.22), channel_id=1, source_target_pairs={{0,4},{1,5},{2,6},{3,7},{4,0},{5,1},{6,2},{7,3},{8,12},{9,13},{10,... | collective-permute-start | bytes 786440 | tf_op jit(solution)/shard_map/ppermute | solution.py:30
  93.5 4.0 %collective-permute-start.13 = (bf16[32,4096]{1,0:T(8,128)(2,1)}, bf16[32,4096]{1,0:T(8,128)(2,1)S(1)}, u32[]{:S(2)}, u32[]{:S(2)}) collective-permute-start(bf16[32,4096]{1,0:T(8,128)(2,1)} %get-tuple-element.23), channel_id=1, source_target_pairs={{0,6},{1,7},{2,0},{3,1},{4,2},{5,3},{6,4},{7,5},{8,14},{9,15},{10,... | collective-permute-start | bytes 786440 | tf_op jit(solution)/shard_map/ppermute | solution.py:30
  97.4 1.9 %collective-permute-start.14 = (bf16[32,4096]{1,0:T(8,128)(2,1)}, bf16[32,4096]{1,0:T(8,128)(2,1)S(1)}, u32[]{:S(2)}, u32[]{:S(2)}) collective-permute-start(bf16[32,4096]{1,0:T(8,128)(2,1)} %get-tuple-element.24), channel_id=1, source_target_pairs={{0,2},{1,3},{2,4},{3,5},{4,6},{5,7},{6,0},{7,1},{8,10},{9,11},{10,... | collective-permute-start | bytes 786440 | tf_op jit(solution)/shard_map/ppermute | solution.py:30
  99.4 6.1 %collective-permute-done.17 = bf16[32,4096]{1,0:T(8,128)(2,1)S(1)} collective-permute-done((bf16[32,4096]{1,0:T(8,128)(2,1)}, bf16[32,4096]{1,0:T(8,128)(2,1)S(1)}, u32[]{:S(2)}, u32[]{:S(2)}) %collective-permute-start.17) | collective-permute-done | bytes 262176 | tf_op jit(solution)/shard_map/ppermute | solution.py:30
  106.6 5.9 %collective-permute-start.18 = (bf16[32,4096]{1,0:T(8,128)(2,1)S(1)}, bf16[32,4096]{1,0:T(8,128)(2,1)S(1)}, u32[]{:S(2)}, u32[]{:S(2)}) collective-permute-start(bf16[32,4096]{1,0:T(8,128)(2,1)S(1)} %add_convert_fusion.1), channel_id=1, source_target_pairs={{0,8},{1,9},{2,10},{3,11},{4,12},{5,13},{6,14},{7,15},{8,0},{9,1},... | collective-permute-start | bytes 786440 | tf_op jit(solution)/shard_map/ppermute | solution.py:30
  112.5 2.3 %fresh.1 = bf16[2,640,128]{2,1,0:T(8,128)(2,1)} custom-call(s32[8,128]{1,0:T(8,128)} %get-tuple-element.29.target_ref, bf16[128,512]{1,0:T(8,128)(2,1)} %get-tuple-element.18.kva_ref, bf16[128,512]{1,0:T(8,128)(2,1)} %get-tuple-element.19.kvb_ref, bf16[128,512]{1,0:T(8,128)(2,1)} %copy-done.2, bf16[128,512]{1,0:T(8,128)(2,1)} %copy-done.1), custom_call_target="tpu_custom_call" | custom-call | flops 167772160 | bytes 2000000 | tf_op jit(solution)/shard_map/fresh/pallas_call | solution.py:278
  114.8 7.9 %collective-permute-done.18 = bf16[32,4096]{1,0:T(8,128)(2,1)S(1)} collective-permute-done((bf16[32,4096]{1,0:T(8,128)(2,1)S(1)}, bf16[32,4096]{1,0:T(8,128)(2,1)S(1)}, u32[]{:S(2)}, u32[]{:S(2)}) %collective-permute-start.18) | collective-permute-done | bytes 262176 | tf_op jit(solution)/shard_map/ppermute | solution.py:30
  (38 shorter events, 12.7 us)
Async XLA Ops:
  0.6 50.0 %collective-permute-start.3 = (bf16[4096,384]{1,0:T(8,128)(2,1)}, bf16[4096,384]{1,0:T(8,128)(2,1)S(1)}, u32[]{:S(2)}, u32[]{:S(2)}) collective-permute-start(bf16[4096,384]{1,0:T(8,128)(2,1)} %mine_ref.4), channel_id=1, source_target_pairs={{0,1},{1,0},{2,3},{3,2},{4,5},{5,4},{6,7},{7,6},{8,9},{9,8},{10,11... | collective-permute-start | bytes 9437192 | tf_op jit(solution)/shard_map/ppermute | solution.py:30
  2.6 70.1 %collective-permute-start.11 = (bf16[128,4096]{1,0:T(8,128)(2,1)}, bf16[128,4096]{1,0:T(8,128)(2,1)}, u32[]{:S(2)}, u32[]{:S(2)}) collective-permute-start(bf16[128,4096]{1,0:T(8,128)(2,1)} %out_mine_ref.1), channel_id=1, source_target_pairs={{0,1},{1,0},{2,3},{3,2},{4,5},{5,4},{6,7},{7,6},{8,9},{9,8},{10,11... | collective-permute-start | bytes 3145736 | tf_op jit(solution)/shard_map/ppermute | solution.py:30
  5.0 19.6 %collective-permute-start.4 = (bf16[32,4096]{1,0:T(8,128)(2,1)}, bf16[32,4096]{1,0:T(8,128)(2,1)S(1)}, u32[]{:S(2)}, u32[]{:S(2)}) collective-permute-start(bf16[32,4096]{1,0:T(8,128)(2,1)} %a_ref.1), channel_id=1, source_target_pairs={{0,8},{1,9},{2,10},{3,11},{4,12},{5,13},{6,14},{7,15},{8,0},{9,1},... | collective-permute-start | bytes 786440 | tf_op jit(solution)/shard_map/ppermute | solution.py:30
  24.6 26.0 %copy-start.4 = (bf16[32,4096]{1,0:T(8,128)(2,1)}, bf16[32,4096]{1,0:T(8,128)(2,1)S(1)}, u32[]{:S(2)}) copy-start(bf16[32,4096]{1,0:T(8,128)(2,1)S(1)} %collective-permute-done.4.a_ref) | copy-start | bytes 786436
  24.6 16.9 %collective-permute-start.5 = (bf16[32,4096]{1,0:T(8,128)(2,1)S(1)}, bf16[32,4096]{1,0:T(8,128)(2,1)S(1)}, u32[]{:S(2)}, u32[]{:S(2)}) collective-permute-start(bf16[32,4096]{1,0:T(8,128)(2,1)S(1)} %collective-permute-done.4.a_ref), channel_id=1, source_target_pairs={{0,2},{1,3},{2,4},{3,5},{4,6},{5,7},{6,0},{7,1},{8,10},{9,11},{10,... | collective-permute-start | bytes 786440 | tf_op jit(solution)/shard_map/ppermute | solution.py:30
  28.3 15.2 %collective-permute-start.6 = (bf16[32,4096]{1,0:T(8,128)(2,1)S(1)}, bf16[32,4096]{1,0:T(8,128)(2,1)S(1)}, u32[]{:S(2)}, u32[]{:S(2)}) collective-permute-start(bf16[32,4096]{1,0:T(8,128)(2,1)S(1)} %collective-permute-done.4.a_ref), channel_id=1, source_target_pairs={{0,4},{1,5},{2,6},{3,7},{4,0},{5,1},{6,2},{7,3},{8,12},{9,13},{10,... | collective-permute-start | bytes 786440 | tf_op jit(solution)/shard_map/ppermute | solution.py:30
  32.9 13.5 %collective-permute-start.7 = (bf16[32,4096]{1,0:T(8,128)(2,1)S(1)}, bf16[32,4096]{1,0:T(8,128)(2,1)S(1)}, u32[]{:S(2)}, u32[]{:S(2)}) collective-permute-start(bf16[32,4096]{1,0:T(8,128)(2,1)S(1)} %collective-permute-done.4.a_ref), channel_id=1, source_target_pairs={{0,6},{1,7},{2,0},{3,1},{4,2},{5,3},{6,4},{7,5},{8,14},{9,15},{10,... | collective-permute-start | bytes 786440 | tf_op jit(solution)/shard_map/ppermute | solution.py:30
  41.6 9.1 %copy-start.5 = (bf16[32,4096]{1,0:T(8,128)(2,1)}, bf16[32,4096]{1,0:T(8,128)(2,1)S(1)}, u32[]{:S(2)}) copy-start(bf16[32,4096]{1,0:T(8,128)(2,1)S(1)} %collective-permute-done.5.b_ref) | copy-start | bytes 786436
  41.6 18.4 %collective-permute-start = (bf16[32,4096]{1,0:T(8,128)(2,1)}, bf16[32,4096]{1,0:T(8,128)(2,1)}, u32[]{:S(2)}, u32[]{:S(2)}) collective-permute-start(bf16[32,4096]{1,0:T(8,128)(2,1)} %a_ref.1), channel_id=1, source_target_pairs={{0,2},{1,3},{2,4},{3,5},{4,6},{5,7},{6,0},{7,1},{8,10},{9,11},{10,... | collective-permute-start | bytes 786440 | tf_op jit(solution)/shard_map/ppermute | solution.py:30
  43.5 7.1 %copy-start.6 = (bf16[32,4096]{1,0:T(8,128)(2,1)}, bf16[32,4096]{1,0:T(8,128)(2,1)S(1)}, u32[]{:S(2)}) copy-start(bf16[32,4096]{1,0:T(8,128)(2,1)S(1)} %collective-permute-done.6.c_ref) | copy-start | bytes 786436
  43.5 18.8 %collective-permute-start.1 = (bf16[32,4096]{1,0:T(8,128)(2,1)}, bf16[32,4096]{1,0:T(8,128)(2,1)}, u32[]{:S(2)}, u32[]{:S(2)}) collective-permute-start(bf16[32,4096]{1,0:T(8,128)(2,1)} %a_ref.1), channel_id=1, source_target_pairs={{0,4},{1,5},{2,6},{3,7},{4,0},{5,1},{6,2},{7,3},{8,12},{9,13},{10,... | collective-permute-start | bytes 786440 | tf_op jit(solution)/shard_map/ppermute | solution.py:30
  46.5 4.2 %copy-start.7 = (bf16[32,4096]{1,0:T(8,128)(2,1)}, bf16[32,4096]{1,0:T(8,128)(2,1)S(1)}, u32[]{:S(2)}) copy-start(bf16[32,4096]{1,0:T(8,128)(2,1)S(1)} %collective-permute-done.7.d_ref) | copy-start | bytes 786436
  46.5 15.9 %collective-permute-start.2 = (bf16[32,4096]{1,0:T(8,128)(2,1)}, bf16[32,4096]{1,0:T(8,128)(2,1)}, u32[]{:S(2)}, u32[]{:S(2)}) collective-permute-start(bf16[32,4096]{1,0:T(8,128)(2,1)} %a_ref.1), channel_id=1, source_target_pairs={{0,6},{1,7},{2,0},{3,1},{4,2},{5,3},{6,4},{7,5},{8,14},{9,15},{10,... | collective-permute-start | bytes 786440 | tf_op jit(solution)/shard_map/ppermute | solution.py:30
  50.6 3.2 %copy-start = (bf16[4096,384]{1,0:T(8,128)(2,1)}, bf16[4096,384]{1,0:T(8,128)(2,1)S(1)}, u32[]{:S(2)}) copy-start(bf16[4096,384]{1,0:T(8,128)(2,1)S(1)} %collective-permute-done.3.other_ref) | copy-start | bytes 9437188
  50.6 22.0 %collective-permute-start.10 = (bf16[2,1,48,16,128]{4,3,2,1,0:T(8,128)(2,1)}, bf16[2,1,48,16,128]{4,3,2,1,0:T(8,128)(2,1)S(1)}, u32[]{:S(2)}, u32[]{:S(2)}) collective-permute-start(bf16[2,1,48,16,128]{4,3,2,1,0:T(8,128)(2,1)} %mine_ref.5), channel_id=1, source_target_pairs={{0,1},{1,0},{2,3},{3,2},{4,5},{5,4},{6,7},{7,6},{8,9},{9,8},{10,11... | collective-permute-start | bytes 1179656 | tf_op jit(solution)/shard_map/ppermute | solution.py:30
  59.9 12.8 %collective-permute-start.9 = (bf16[128,512]{1,0:T(8,128)(2,1)}, bf16[128,512]{1,0:T(8,128)(2,1)S(1)}, u32[]{:S(2)}, u32[]{:S(2)}) collective-permute-start(bf16[128,512]{1,0:T(8,128)(2,1)} %get-tuple-element.19.kvb_ref), channel_id=1, source_target_pairs={{0,1},{1,0},{2,3},{3,2},{4,5},{5,4},{6,7},{7,6},{8,9},{9,8},{10,11... | collective-permute-start | bytes 393224 | tf_op jit(solution)/shard_map/ppermute | solution.py:30
  68.4 4.3 %collective-permute-start.8 = (bf16[128,512]{1,0:T(8,128)(2,1)}, bf16[128,512]{1,0:T(8,128)(2,1)S(1)}, u32[]{:S(2)}, u32[]{:S(2)}) collective-permute-start(bf16[128,512]{1,0:T(8,128)(2,1)} %get-tuple-element.18.kva_ref), channel_id=1, source_target_pairs={{0,1},{1,0},{2,3},{3,2},{4,5},{5,4},{6,7},{7,6},{8,9},{9,8},{10,11... | collective-permute-start | bytes 393224 | tf_op jit(solution)/shard_map/ppermute | solution.py:30
  80.2 17.2 %collective-permute-start.15 = (bf16[32,4096]{1,0:T(8,128)(2,1)}, bf16[32,4096]{1,0:T(8,128)(2,1)S(1)}, u32[]{:S(2)}, u32[]{:S(2)}) collective-permute-start(bf16[32,4096]{1,0:T(8,128)(2,1)} %get-tuple-element.26), channel_id=1, source_target_pairs={{0,4},{1,5},{2,6},{3,7},{4,0},{5,1},{6,2},{7,3},{8,12},{9,13},{10,... | collective-permute-start | bytes 786440 | tf_op jit(solution)/shard_map/ppermute | solution.py:30
  85.1 14.3 %collective-permute-start.16 = (bf16[32,4096]{1,0:T(8,128)(2,1)}, bf16[32,4096]{1,0:T(8,128)(2,1)S(1)}, u32[]{:S(2)}, u32[]{:S(2)}) collective-permute-start(bf16[32,4096]{1,0:T(8,128)(2,1)} %get-tuple-element.27), channel_id=1, source_target_pairs={{0,6},{1,7},{2,0},{3,1},{4,2},{5,3},{6,4},{7,5},{8,14},{9,15},{10,... | collective-permute-start | bytes 786440 | tf_op jit(solution)/shard_map/ppermute | solution.py:30
  87.6 17.9 %collective-permute-start.17 = (bf16[32,4096]{1,0:T(8,128)(2,1)}, bf16[32,4096]{1,0:T(8,128)(2,1)S(1)}, u32[]{:S(2)}, u32[]{:S(2)}) collective-permute-start(bf16[32,4096]{1,0:T(8,128)(2,1)} %get-tuple-element.28), channel_id=1, source_target_pairs={{0,2},{1,3},{2,4},{3,5},{4,6},{5,7},{6,0},{7,1},{8,10},{9,11},{10,... | collective-permute-start | bytes 786440 | tf_op jit(solution)/shard_map/ppermute | solution.py:30
  90.9 23.9 %collective-permute-start.12 = (bf16[32,4096]{1,0:T(8,128)(2,1)}, bf16[32,4096]{1,0:T(8,128)(2,1)S(1)}, u32[]{:S(2)}, u32[]{:S(2)}) collective-permute-start(bf16[32,4096]{1,0:T(8,128)(2,1)} %get-tuple-element.22), channel_id=1, source_target_pairs={{0,4},{1,5},{2,6},{3,7},{4,0},{5,1},{6,2},{7,3},{8,12},{9,13},{10,... | collective-permute-start | bytes 786440 | tf_op jit(solution)/shard_map/ppermute | solution.py:30
  93.5 21.4 %collective-permute-start.13 = (bf16[32,4096]{1,0:T(8,128)(2,1)}, bf16[32,4096]{1,0:T(8,128)(2,1)S(1)}, u32[]{:S(2)}, u32[]{:S(2)}) collective-permute-start(bf16[32,4096]{1,0:T(8,128)(2,1)} %get-tuple-element.23), channel_id=1, source_target_pairs={{0,6},{1,7},{2,0},{3,1},{4,2},{5,3},{6,4},{7,5},{8,14},{9,15},{10,... | collective-permute-start | bytes 786440 | tf_op jit(solution)/shard_map/ppermute | solution.py:30
  97.4 17.4 %collective-permute-start.14 = (bf16[32,4096]{1,0:T(8,128)(2,1)}, bf16[32,4096]{1,0:T(8,128)(2,1)S(1)}, u32[]{:S(2)}, u32[]{:S(2)}) collective-permute-start(bf16[32,4096]{1,0:T(8,128)(2,1)} %get-tuple-element.24), channel_id=1, source_target_pairs={{0,2},{1,3},{2,4},{3,5},{4,6},{5,7},{6,0},{7,1},{8,10},{9,11},{10,... | collective-permute-start | bytes 786440 | tf_op jit(solution)/shard_map/ppermute | solution.py:30
  106.6 16.2 %collective-permute-start.18 = (bf16[32,4096]{1,0:T(8,128)(2,1)S(1)}, bf16[32,4096]{1,0:T(8,128)(2,1)S(1)}, u32[]{:S(2)}, u32[]{:S(2)}) collective-permute-start(bf16[32,4096]{1,0:T(8,128)(2,1)S(1)} %add_convert_fusion.1), channel_id=1, source_target_pairs={{0,8},{1,9},{2,10},{3,11},{4,12},{5,13},{6,14},{7,15},{8,0},{9,1},... | collective-permute-start | bytes 786440 | tf_op jit(solution)/shard_map/ppermute | solution.py:30
  (3 other events, 2.3 us)

commit v2 on v1

v2 whole, which is shorter than its diff:
```python
import jax
import jax.numpy as jnp
from jax import lax
from jax.experimental import pallas as pl
from jax.experimental.pallas import tpu as pltpu
from jax.sharding import PartitionSpec as P


MODEL_HEADS = 32
N_X = 4
N_TP = 16
BLOCK = 32
PAGE = 16
SEQS = 8
HEAD = 128
FAR = 3e32


def tp_of(y, x, c):
    return (y % 2) * 8 + (x % N_X) * 2 + c % 2


def moved(value, dy, dx, dc):
    pairs = [
        (tp_of(y, x, c), tp_of(y + dy, x + dx, c + dc))
        for y in range(2)
        for x in range(N_X)
        for c in range(2)
    ]
    return lax.ppermute(value, "tp", pairs)


def my_place():
    me = lax.axis_index("tp")
    return me >> 3, (me >> 1) & 3, me & 1


def layout_kernel(*refs):
    sources, (dist_ref, target_ref), held = refs[:7], refs[7:9], refs[9:16]
    sems = refs[16]
    copies = [
        pltpu.make_async_copy(source, place, sems.at[i])
        for i, (source, place) in enumerate(zip(sources, held[3:] + held[:3]))
    ]
    for copy in copies:
        copy.start()
    seg_ref, prefix_ref, order_ref, fresh_ref = held[3:]
    for copy in copies[:4]:
        copy.wait()
    y, x, c = my_place()
    seg = seg_ref[...]
    starts = [jnp.int32(0)]
    for s in range(1, SEQS):
        starts.append(jnp.sum((seg < s).astype(jnp.float32)).astype(jnp.int32))
    ends = starts[1:] + [jnp.int32(seg.shape[0] * seg.shape[1])]
    cache_starts = [jnp.int32(0)]
    fresh_starts = [jnp.int32(0)]
    for s in range(SEQS):
        cache_starts.append(cache_starts[s] + prefix_ref[s])
        fresh_starts.append(fresh_starts[s] + ((ends[s] - starts[s] + PAGE - 1) >> 4))

    def pick(token, values):
        result = jnp.full(token.shape, values[0], jnp.int32)
        for s in range(1, SEQS):
            result = jnp.where(token >= starts[s], values[s], result)
        return result

    row = lax.broadcasted_iota(jnp.int32, (8, 128), 0)
    lane = lax.broadcasted_iota(jnp.int32, (8, 128), 1)
    physical = row * 128 + lane
    page = physical >> 4
    slot = jnp.zeros((8, 128), jnp.int32)
    for i in range(order_ref.shape[0]):
        slot = jnp.where(page == order_ref[i], i * PAGE, slot)
    slot = slot + (physical & (PAGE - 1))
    slot_owner = jnp.zeros((8, 128), jnp.int32)
    for s in range(1, SEQS):
        slot_owner = slot_owner + (slot >= cache_starts[s] * PAGE).astype(jnp.int32)

    yy, cc, dx = row & 1, row >> 1, lane >> 5
    holder = ((y + yy) & 1) * 8 + ((x - dx) & 3) * 2 + ((c + cc) & 1)
    token = holder * BLOCK + (lane & (BLOCK - 1))
    token_owner = pick(token, list(range(SEQS)))
    in_prompt = token - pick(token, starts)
    page_slot = pick(token, fresh_starts[:SEQS]) + (in_prompt >> 4)
    fresh_page = jnp.zeros((8, 128), jnp.int32)
    for i in range(fresh_ref.shape[0]):
        fresh_page = jnp.where(page_slot == i, fresh_ref[i], fresh_page)
    target_ref[...] = fresh_page * PAGE + (in_prompt & (PAGE - 1))

    base = [cache_starts[s + 1] * PAGE - starts[s] for s in range(SEQS)]
    for b in range(8):
        at = ((y + b // 4) & 1) * 8 + ((x - b % 4) & 3) * 2 + c
        query = at * BLOCK + lax.broadcasted_iota(jnp.int32, (BLOCK, 128), 0)
        owner = pick(query, list(range(SEQS)))
        reach = pick(query, base) + query
        rows = slice(b * BLOCK, (b + 1) * BLOCK)
        for k in range(6):
            apart = (reach - slot[k : k + 1, :]).astype(jnp.float32)
            dist_ref[rows, k * 128 : (k + 1) * 128] = jnp.where(
                owner == slot_owner[k : k + 1, :], apart, FAR
            )
        for k in range(4):
            gap = query - token[k : k + 1, :]
            usable = (owner == token_owner[k : k + 1, :]) & (gap >= 0)
            dist_ref[rows, (6 + k) * 128 : (7 + k) * 128] = jnp.where(
                usable, gap.astype(jnp.float32), FAR
            )
    for copy in copies[4:]:
        copy.wait()


def in_vmem(value):
    return pltpu.with_memory_space_constraint(value, pltpu.VMEM)


def in_hbm(value):
    return pltpu.with_memory_space_constraint(value, pltpu.HBM)


def layout_tables(segment_ids, prefix_pages, page_order, fresh_order, gain, tokens, weight):
    vmem = pl.BlockSpec(memory_space=pltpu.VMEM)
    kept = (gain, tokens, weight)
    small = (prefix_pages, page_order, fresh_order)
    return pl.pallas_call(
        layout_kernel,
        out_shape=[
            jax.ShapeDtypeStruct((256, 1280), jnp.float32),
            jax.ShapeDtypeStruct((8, 128), jnp.int32),
        ]
        + [jax.ShapeDtypeStruct(value.shape, value.dtype) for value in kept],
        in_specs=[pl.BlockSpec(memory_space=pltpu.HBM)] * 7,
        out_specs=[vmem] * 5,
        scratch_shapes=[pltpu.VMEM((4, 128), jnp.int32)]
        + [pltpu.SMEM(value.shape, jnp.int32) for value in small]
        + [pltpu.SemaphoreType.DMA((7,))],
        compiler_params=pltpu.CompilerParams(vmem_limit_bytes=12 * 2**20),
        cost_estimate=pl.CostEstimate(flops=0, bytes_accessed=6_000_000, transcendentals=0),
        name="layout",
    )(*[in_hbm(value) for value in (segment_ids.reshape(4, 128), *small, *kept)])


def project_kernel(*refs):
    pieces, (gain_ref, mine_ref, other_ref, q_ref, kv_ref, normed) = refs[:8], refs[8:]
    gain = jnp.concatenate([gain_ref[k : k + 1, :] for k in range(gain_ref.shape[0])], axis=1)
    gain = gain.astype(jnp.float32)
    for i, ref in enumerate(pieces):
        for h in range(2):
            values = ref[h * 16 : (h + 1) * 16, :].astype(jnp.float32)
            center = values - jnp.mean(values, axis=-1, keepdims=True)
            spread = jnp.mean(center * center, axis=-1, keepdims=True)
            normed[i * BLOCK + h * 16 : i * BLOCK + (h + 1) * 16, :] = (
                center * lax.rsqrt(spread + 1e-05) * gain
            ).astype(jnp.bfloat16)
    left = normed[...]

    def times(right):
        return jnp.dot(left, right, preferred_element_type=jnp.float32).astype(jnp.bfloat16)

    first = times(mine_ref[:, :256])
    q_ref[:, :128] = first[:, :128]
    kv_ref[:, :128] = first[:, 128:]
    middle = times(jnp.concatenate([mine_ref[:, 256:], other_ref[:, :128]], axis=1))
    kv_ref[:, 128:256] = middle[:, :128]
    q_ref[:, 128:] = middle[:, 128:]
    kv_ref[:, 256:] = times(other_ref[:, 128:])


def project(pieces, gain, mine, other):
    vmem = pl.BlockSpec(memory_space=pltpu.VMEM)
    return pl.pallas_call(
        project_kernel,
        out_shape=(
            jax.ShapeDtypeStruct((256, 256), jnp.bfloat16),
            jax.ShapeDtypeStruct((256, 512), jnp.bfloat16),
        ),
        in_specs=[vmem] * 11,
        out_specs=(vmem, vmem),
        scratch_shapes=[pltpu.VMEM((256, 4096), jnp.bfloat16)],
        compiler_params=pltpu.CompilerParams(vmem_limit_bytes=24 * 2**20),
        cost_estimate=pl.CostEstimate(
            flops=2 * 256 * 4096 * 768, bytes_accessed=9_000_000, transcendentals=0
        ),
        name="project",
    )(*[in_vmem(piece) for piece in pieces], in_vmem(gain), in_vmem(mine), in_vmem(other))


def out_rows(left, right, mine_ref, other_ref, out_refs):
    for n in range(8):
        lanes = slice(n * 512, (n + 1) * 512)
        partial = (
            jnp.dot(left, mine_ref[:, lanes], preferred_element_type=jnp.float32)
            + jnp.dot(right, other_ref[:, lanes], preferred_element_type=jnp.float32)
        ).astype(jnp.bfloat16)
        for i, out_ref in enumerate(out_refs):
            out_ref[:, lanes] = partial[i * BLOCK : (i + 1) * BLOCK]


def attend_kernel(
    q_ref, near_ref, mine_ref, dist_ref, away_ref, other_ref, out_mine_ref, out_other_ref, *rest,
):
    out_refs, (scores, weights, context_ref) = rest[:8], rest[8:]
    y, x, c = my_place()
    cached = (mine_ref, other_ref)
    turned = (((1,), (1,)), ((), ()))
    log2e = 1.4426950408889634
    for head in range(2):
        columns = slice(head * HEAD, (head + 1) * HEAD)
        at = (y * 8 + x * 2 + (c ^ head) + 1).astype(jnp.float32)
        slope = log2e * jnp.exp2(
            jnp.full((1, 128), -8.0 * (MODEL_HEADS // N_TP) / MODEL_HEADS, jnp.float32) * at
        )
        q = q_ref[:, columns]
        new = ((near_ref, head * 256), (away_ref, (1 - head) * 256))
        scores[:, :768] = lax.dot_general(
            q, cached[head][0, 0].reshape(768, HEAD), turned, preferred_element_type=jnp.float32
        )
        for i, (ref, first) in enumerate(new):
            scores[:, 768 + i * 256 : 1024 + i * 256] = lax.dot_general(
                q, ref[:, first : first + HEAD], turned, preferred_element_type=jnp.float32
            )
        sums = []
        for b in range(8):
            rows = slice(b * BLOCK, (b + 1) * BLOCK)
            pieces = []
            peak = None
            for k in range(10):
                lanes = slice(k * 128, (k + 1) * 128)
                piece = scores[rows, lanes] * (log2e * HEAD ** (-0.5)) - slope * dist_ref[rows, lanes]
                peak = piece if peak is None else jnp.maximum(peak, piece)
                pieces.append(piece)
            peak = jnp.max(peak, axis=1, keepdims=True)
            total = None
            for k in range(10):
                weight = jnp.exp2(pieces[k] - peak)
                total = weight if total is None else total + weight
                weights[rows, k * 128 : (k + 1) * 128] = weight.astype(jnp.bfloat16)
            sums.append(jnp.sum(total, axis=1, keepdims=True))
        result = jnp.dot(
            weights[:, :768], cached[head][1, 0].reshape(768, HEAD), preferred_element_type=jnp.float32
        )
        for i, (ref, first) in enumerate(new):
            result = result + jnp.dot(
                weights[:, 768 + i * 256 : 1024 + i * 256],
                ref[:, first + HEAD : first + 2 * HEAD],
                preferred_element_type=jnp.float32,
            )
        for b in range(8):
            context_ref[b * BLOCK : (b + 1) * BLOCK, columns] = (
                result[b * BLOCK : (b + 1) * BLOCK] / sums[b]
            ).astype(jnp.bfloat16)
    out_rows(context_ref[:, :HEAD], context_ref[:, HEAD:], out_mine_ref, out_other_ref, out_refs)


def attend(queries, near, away, mine, other, dist, out_mine, out_other):
    vmem = pl.BlockSpec(memory_space=pltpu.VMEM)
    operands = (queries, near, mine, dist, away, other, out_mine, out_other)
    return pl.pallas_call(
        attend_kernel,
        out_shape=[jax.ShapeDtypeStruct((BLOCK, 4096), jnp.bfloat16)] * 8,
        in_specs=[vmem] * 8,
        out_specs=[vmem] * 8,
        scratch_shapes=[
            pltpu.VMEM((256, 1280), jnp.float32),
            pltpu.VMEM((256, 1280), jnp.bfloat16),
            pltpu.VMEM((256, 256), jnp.bfloat16),
        ],
        compiler_params=pltpu.CompilerParams(vmem_limit_bytes=24 * 2**20),
        cost_estimate=pl.CostEstimate(
            flops=4 * 256 * 1280 * 256 + 2 * 256 * 256 * 4096,
            bytes_accessed=8_000_000,
            transcendentals=2 * 256 * 1280,
        ),
        name="attend",
    )(*[in_vmem(operand) for operand in operands])


def fresh_kernel(target_ref, near_ref, away_ref, out_ref):
    total = out_ref.shape[1]
    places = lax.broadcasted_iota(jnp.int32, (total, 128), 0)
    result = None
    for i in range(4):
        rows = slice((i & 1) * 128, (i & 1) * 128 + 128)
        piece = near_ref[rows, :256] if i < 2 else away_ref[rows, 256:]
        chosen = (places == target_ref[i : i + 1, :]).astype(jnp.float32).astype(jnp.bfloat16)
        part = jnp.dot(chosen, piece, preferred_element_type=jnp.float32)
        result = part if result is None else result + part
    out_ref[0] = result[:, :HEAD].astype(jnp.bfloat16)
    out_ref[1] = result[:, HEAD:].astype(jnp.bfloat16)


def fresh(target, near, away, pages):
    vmem = pl.BlockSpec(memory_space=pltpu.VMEM)
    return pl.pallas_call(
        fresh_kernel,
        out_shape=jax.ShapeDtypeStruct((2, pages * PAGE, HEAD), jnp.bfloat16),
        in_specs=[vmem] * 3,
        out_specs=vmem,
        compiler_params=pltpu.CompilerParams(vmem_limit_bytes=12 * 2**20),
        cost_estimate=pl.CostEstimate(
            flops=2 * 640 * 512 * 256, bytes_accessed=2_000_000, transcendentals=0
        ),
        name="fresh",
    )(target, near, away)


def body(
    tokens,
    norm_gain,
    qkv_weight,
    out_weight,
    segment_ids,
    prefix_pages,
    page_order,
    fresh_order,
    cache_pool,
):
    def added(values):
        total = values[0].astype(jnp.float32)
        for value in values[1:]:
            total = total + value.astype(jnp.float32)
        return total

    partner = moved(tokens, 1, 0, 0)
    qkv_other = moved(qkv_weight, 0, 0, 1)
    cache_other = moved(cache_pool, 0, 0, 1)
    out_other = moved(out_weight, 0, 0, 1)
    own, across = [tokens], [partner]
    for dx in (1, 2, 3):
        own.append(moved(tokens, 0, dx, 0))
        across.append(moved(partner, 0, dx, 0))
    dist, target, gain, own[0], qkv_mine = layout_tables(
        segment_ids, prefix_pages, page_order, fresh_order,
        norm_gain.reshape(32, 128), tokens, qkv_weight,
    )
    queries, near = project(own + across, gain, qkv_mine, qkv_other)
    away = moved(near, 0, 0, 1)
    partial = attend(queries, near, away, cache_pool, cache_other, dist, out_weight, out_other)
    kept, passed = partial[:4], partial[4:]
    passed_in = [passed[0]]
    for dx in (1, 2, 3):
        passed_in.append(moved(passed[dx], 0, -dx, 0))
    kept_in = [kept[0]]
    for dx in (1, 2, 3):
        kept_in.append(moved(kept[dx], 0, -dx, 0))
    passed_sum = added(passed_in).astype(jnp.bfloat16)
    from_partner = moved(passed_sum, 1, 0, 0)
    fresh_pages = fresh(target, near, away, fresh_order.shape[0])
    kept_sum = lax.optimization_barrier(added([kept_in[0], kept_in[1], kept_in[3]]))
    summed = added([kept_sum, kept_in[2], from_partner]).astype(jnp.bfloat16)
    return (summed, fresh_pages.reshape(2, 1, fresh_order.shape[0], PAGE, HEAD))


def solution(mesh):
    placed = (
        P(("req", "tp"), None),
        P(),
        P(None, "tp"),
        P("tp", None),
        P("req"),
        P("req"),
        P("req"),
        P("req"),
        P(None, "tp", "req", None, None),
    )
    return jax.shard_map(
        body,
        mesh=mesh,
        in_specs=placed,
        out_specs=(P(("req", "tp"), None), P(None, "tp", "req", None, None)),
        check_vma=False,
    )
```

time: 125 us -> 101 us (0.81)
  the two profiles are of different devices: /device:TPU:32 before, /device:TPU:1 now
where the time goes in v2:
time: 101 us
  starting transfers between devices  63 us (62%)
  waiting for transfers between devices  26.6 us (26%)
  Pallas kernels  9.07 us (9%)
    ppermute x18, starting transfers between devices, moved(): return lax.ppermute(value, 'tp', pairs)  63 us
    ppermute x18, waiting for transfers between devices, moved(): return lax.ppermute(value, 'tp', pairs)  26.6 us
    pallas_call x1, Pallas kernels, attend(): pl.pallas_call(attend_kernel, out_shape=[jax.ShapeDtypeStruct((BLOCK, 409...  2.9 us
    pallas_call x1, Pallas kernels, project(): pl.pallas_call(project_kernel, out_shape=(jax.ShapeDtypeStruct((256, 256)...  2.89 us
    pallas_call x1, Pallas kernels, layout_tables(): pl.pallas_call(layout_kernel, out_shape=[jax.ShapeDtypeStruct((256, 1280)...  2.08 us
  transfers between devices with their start and end apart: 18, of which 7 were waited for; matrix products, arithmetic and copies ran while one was open for 0% of the time, Pallas kernels for 6%

profile of v2, /device:TPU:1, one launch (start us, length us, event | category | flops | bytes accessed | tf_op | source)
XLA Modules:
  0.0 100.5 jit_solution(13034450568885764299)
XLA Ops:
  0.6 8.9 %collective-permute-start.7 = (bf16[4096,384]{1,0:T(8,128)(2,1)}, bf16[4096,384]{1,0:T(8,128)(2,1)S(1)}, u32[]{:S(2)}, u32[]{:S(2)}) collective-permute-start(bf16[4096,384]{1,0:T(8,128)(2,1)} %refs_6_.1), channel_id=1, source_target_pairs={{0,1},{1,0},{2,3},{3,2},{4,5},{5,4},{6,7},{7,6},{8,9},{9,8},{10,11... | collective-permute-start | bytes 9437192 | tf_op jit(solution)/shard_map/ppermute | solution.py:30
  9.5 2.1 %collective-permute-start.3 = (bf16[32,4096]{1,0:T(8,128)(2,1)}, bf16[32,4096]{1,0:T(8,128)(2,1)S(1)}, u32[]{:S(2)}, u32[]{:S(2)}) collective-permute-start(bf16[32,4096]{1,0:T(8,128)(2,1)} %refs_5_.1), channel_id=1, source_target_pairs={{0,8},{1,9},{2,10},{3,11},{4,12},{5,13},{6,14},{7,15},{8,0},{9,1},... | collective-permute-start | bytes 786440 | tf_op jit(solution)/shard_map/ppermute | solution.py:30
  11.6 2.2 %collective-permute-start.10 = (bf16[128,4096]{1,0:T(8,128)(2,1)}, bf16[128,4096]{1,0:T(8,128)(2,1)S(1)}, u32[]{:S(2)}, u32[]{:S(2)}) collective-permute-start(bf16[128,4096]{1,0:T(8,128)(2,1)} %out_mine_ref.1), channel_id=1, source_target_pairs={{0,1},{1,0},{2,3},{3,2},{4,5},{5,4},{6,7},{7,6},{8,9},{9,8},{10,11... | collective-permute-start | bytes 3145736 | tf_op jit(solution)/shard_map/ppermute | solution.py:30
  13.9 3.1 %collective-permute-start = (bf16[32,4096]{1,0:T(8,128)(2,1)}, bf16[32,4096]{1,0:T(8,128)(2,1)S(1)}, u32[]{:S(2)}, u32[]{:S(2)}) collective-permute-start(bf16[32,4096]{1,0:T(8,128)(2,1)} %refs_5_.1), channel_id=1, source_target_pairs={{0,2},{1,3},{2,4},{3,5},{4,6},{5,7},{6,0},{7,1},{8,10},{9,11},{10,... | collective-permute-start | bytes 786440 | tf_op jit(solution)/shard_map/ppermute | solution.py:30
  17.0 4.4 %collective-permute-start.1 = (bf16[32,4096]{1,0:T(8,128)(2,1)}, bf16[32,4096]{1,0:T(8,128)(2,1)S(1)}, u32[]{:S(2)}, u32[]{:S(2)}) collective-permute-start(bf16[32,4096]{1,0:T(8,128)(2,1)} %refs_5_.1), channel_id=1, source_target_pairs={{0,4},{1,5},{2,6},{3,7},{4,0},{5,1},{6,2},{7,3},{8,12},{9,13},{10,... | collective-permute-start | bytes 786440 | tf_op jit(solution)/shard_map/ppermute | solution.py:30
  21.3 6.4 %collective-permute-done.3.refs_4_ = bf16[32,4096]{1,0:T(8,128)(2,1)S(1)} collective-permute-done((bf16[32,4096]{1,0:T(8,128)(2,1)}, bf16[32,4096]{1,0:T(8,128)(2,1)S(1)}, u32[]{:S(2)}, u32[]{:S(2)}) %collective-permute-start.3) | collective-permute-done | bytes 262176 | tf_op jit(solution)/shard_map/ppermute | solution.py:30
  29.7 3.4 %collective-permute-start.4 = (bf16[32,4096]{1,0:T(8,128)(2,1)S(1)}, bf16[32,4096]{1,0:T(8,128)(2,1)S(1)}, u32[]{:S(2)}, u32[]{:S(2)}) collective-permute-start(bf16[32,4096]{1,0:T(8,128)(2,1)S(1)} %collective-permute-done.3.refs_4_), channel_id=1, source_target_pairs={{0,2},{1,3},{2,4},{3,5},{4,6},{5,7},{6,0},{7,1},{8,10},{9,11},{10,... | collective-permute-start | bytes 786440 | tf_op jit(solution)/shard_map/ppermute | solution.py:30
  35.0 2.3 %collective-permute-done.2.refs_3_ = bf16[32,4096]{1,0:T(8,128)(2,1)S(1)} collective-permute-done((bf16[32,4096]{1,0:T(8,128)(2,1)}, bf16[32,4096]{1,0:T(8,128)(2,1)S(1)}, u32[]{:S(2)}, u32[]{:S(2)}) %collective-permute-start.2) | collective-permute-done | bytes 262176 | tf_op jit(solution)/shard_map/ppermute | solution.py:30
  37.3 3.4 %collective-permute-start.6 = (bf16[32,4096]{1,0:T(8,128)(2,1)S(1)}, bf16[32,4096]{1,0:T(8,128)(2,1)S(1)}, u32[]{:S(2)}, u32[]{:S(2)}) collective-permute-start(bf16[32,4096]{1,0:T(8,128)(2,1)S(1)} %collective-permute-done.3.refs_4_), channel_id=1, source_target_pairs={{0,6},{1,7},{2,0},{3,1},{4,2},{5,3},{6,4},{7,5},{8,14},{9,15},{10,... | collective-permute-start | bytes 786440 | tf_op jit(solution)/shard_map/ppermute | solution.py:30
  40.7 2.1 %layout.1 = (f32[256,1280]{1,0:T(8,128)S(1)}, s32[8,128]{1,0:T(8,128)S(1)}, bf16[32,128]{1,0:T(8,128)(2,1)S(1)}, bf16[32,4096]{1,0:T(8,128)(2,1)S(1)}, bf16[4096,384]{1,0:T(8,128)(2,1)S(1)}) custom-call(s32[4,128]{1,0:T(4,128)} %bitcast.7, s32[8]{0:T(128)} %refs_1_.1, s32[48]{0:T(128)} %refs_2_.1, s32[40]{0:T(128)} %refs_3_.1, bf16[32,128]{1,0:T(8,128)(2,1)} %bitcast.6, ...), custom_call_target="tpu_custom_call" | custom-call | bytes 6000000 | tf_op jit(solution)/shard_map/layout/pallas_call | solution.py:125
  42.8 3.1 %collective-permute-done.4.refs_5_ = bf16[32,4096]{1,0:T(8,128)(2,1)S(1)} collective-permute-done((bf16[32,4096]{1,0:T(8,128)(2,1)S(1)}, bf16[32,4096]{1,0:T(8,128)(2,1)S(1)}, u32[]{:S(2)}, u32[]{:S(2)}) %collective-permute-start.4) | collective-permute-done | bytes 262176 | tf_op jit(solution)/shard_map/ppermute | solution.py:30
  45.9 3.2 %collective-permute-start.9 = (bf16[2,1,48,16,128]{4,3,2,1,0:T(8,128)(2,1)S(1)}, bf16[2,1,48,16,128]{4,3,2,1,0:T(8,128)(2,1)S(1)}, u32[]{:S(2)}, u32[]{:S(2)}) collective-permute-start(bf16[2,1,48,16,128]{4,3,2,1,0:T(8,128)(2,1)S(1)} %copy-done.1), channel_id=1, source_target_pairs={{0,1},{1,0},{2,3},{3,2},{4,5},{5,4},{6,7},{7,6},{8,9},{9,8},{10,11... | collective-permute-start | bytes 1179656 | tf_op jit(solution)/shard_map/ppermute | solution.py:30
  49.1 2.9 %project.1 = (bf16[256,256]{1,0:T(8,128)(2,1)S(1)}, bf16[256,512]{1,0:T(8,128)(2,1)S(1)}) custom-call(bf16[32,4096]{1,0:T(8,128)(2,1)S(1)} %get-tuple-element.17.refs_0_, bf16[32,4096]{1,0:T(8,128)(2,1)S(1)} %collective-permute-done.refs_1_, bf16[32,4096]{1,0:T(8,128)(2,1)S(1)} %collective-permute-done.1.refs_2_, ...), custom_call_target="tpu_custom_call" | custom-call | flops 1610612736 | bytes 9000000 | tf_op jit(solution)/shard_map/project/pallas_call | solution.py:171
  52.0 2.6 %collective-permute-start.8 = (bf16[256,512]{1,0:T(8,128)(2,1)S(1)}, bf16[256,512]{1,0:T(8,128)(2,1)S(1)}, u32[]{:S(2)}, u32[]{:S(2)}) collective-permute-start(bf16[256,512]{1,0:T(8,128)(2,1)S(1)} %get-tuple-element.21.near_ref), channel_id=1, source_target_pairs={{0,1},{1,0},{2,3},{3,2},{4,5},{5,4},{6,7},{7,6},{8,9},{9,8},{10,11... | collective-permute-start | bytes 786440 | tf_op jit(solution)/shard_map/ppermute | solution.py:30
  55.8 2.9 %attend.1 = (bf16[32,4096]{1,0:T(8,128)(2,1)S(1)}, bf16[32,4096]{1,0:T(8,128)(2,1)S(1)}, bf16[32,4096]{1,0:T(8,128)(2,1)S(1)}, bf16[32,4096]{1,0:T(8,128)(2,1)S(...) custom-call(bf16[256,256]{1,0:T(8,128)(2,1)S(1)} %get-tuple-element., ...), custom_call_target="tpu_custom_call" | custom-call | flops 872415232 | bytes 8000000 | tf_op jit(solution)/shard_map/attend/pallas_call | solution.py:258
  58.7 4.3 %collective-permute-start.14 = (bf16[32,4096]{1,0:T(8,128)(2,1)S(1)}, bf16[32,4096]{1,0:T(8,128)(2,1)S(1)}, u32[]{:S(2)}, u32[]{:S(2)}) collective-permute-start(bf16[32,4096]{1,0:T(8,128)(2,1)S(1)} %get-tuple-element.28), channel_id=1, source_target_pairs={{0,6},{1,7},{2,0},{3,1},{4,2},{5,3},{6,4},{7,5},{8,14},{9,15},{10,... | collective-permute-start | bytes 786440 | tf_op jit(solution)/shard_map/ppermute | solution.py:30
  63.0 2.3 %collective-permute-start.15 = (bf16[32,4096]{1,0:T(8,128)(2,1)S(1)}, bf16[32,4096]{1,0:T(8,128)(2,1)S(1)}, u32[]{:S(2)}, u32[]{:S(2)}) collective-permute-start(bf16[32,4096]{1,0:T(8,128)(2,1)S(1)} %get-tuple-element.29), channel_id=1, source_target_pairs={{0,4},{1,5},{2,6},{3,7},{4,0},{5,1},{6,2},{7,3},{8,12},{9,13},{10,... | collective-permute-start | bytes 786440 | tf_op jit(solution)/shard_map/ppermute | solution.py:30
  65.3 2.1 %collective-permute-start.16 = (bf16[32,4096]{1,0:T(8,128)(2,1)S(1)}, bf16[32,4096]{1,0:T(8,128)(2,1)S(1)}, u32[]{:S(2)}, u32[]{:S(2)}) collective-permute-start(bf16[32,4096]{1,0:T(8,128)(2,1)S(1)} %get-tuple-element.30), channel_id=1, source_target_pairs={{0,2},{1,3},{2,4},{3,5},{4,6},{5,7},{6,0},{7,1},{8,10},{9,11},{10,... | collective-permute-start | bytes 786440 | tf_op jit(solution)/shard_map/ppermute | solution.py:30
  67.4 4.4 %collective-permute-start.11 = (bf16[32,4096]{1,0:T(8,128)(2,1)S(1)}, bf16[32,4096]{1,0:T(8,128)(2,1)S(1)}, u32[]{:S(2)}, u32[]{:S(2)}) collective-permute-start(bf16[32,4096]{1,0:T(8,128)(2,1)S(1)} %get-tuple-element.24), channel_id=1, source_target_pairs={{0,6},{1,7},{2,0},{3,1},{4,2},{5,3},{6,4},{7,5},{8,14},{9,15},{10,... | collective-permute-start | bytes 786440 | tf_op jit(solution)/shard_map/ppermute | solution.py:30
  75.0 3.2 %collective-permute-start.13 = (bf16[32,4096]{1,0:T(8,128)(2,1)S(1)}, bf16[32,4096]{1,0:T(8,128)(2,1)S(1)}, u32[]{:S(2)}, u32[]{:S(2)}) collective-permute-start(bf16[32,4096]{1,0:T(8,128)(2,1)S(1)} %get-tuple-element.26), channel_id=1, source_target_pairs={{0,4},{1,5},{2,6},{3,7},{4,0},{5,1},{6,2},{7,3},{8,12},{9,13},{10,... | collective-permute-start | bytes 786440 | tf_op jit(solution)/shard_map/ppermute | solution.py:30
  78.2 2.0 %collective-permute-done.16 = bf16[32,4096]{1,0:T(8,128)(2,1)S(1)} collective-permute-done((bf16[32,4096]{1,0:T(8,128)(2,1)S(1)}, bf16[32,4096]{1,0:T(8,128)(2,1)S(1)}, u32[]{:S(2)}, u32[]{:S(2)}) %collective-permute-start.16) | collective-permute-done | bytes 262176 | tf_op jit(solution)/shard_map/ppermute | solution.py:30
  80.4 7.6 %collective-permute-start.17 = (bf16[32,4096]{1,0:T(8,128)(2,1)S(1)}, bf16[32,4096]{1,0:T(8,128)(2,1)S(1)}, u32[]{:S(2)}, u32[]{:S(2)}) collective-permute-start(bf16[32,4096]{1,0:T(8,128)(2,1)S(1)} %add_convert_fusion.1), channel_id=1, source_target_pairs={{0,8},{1,9},{2,10},{3,11},{4,12},{5,13},{6,14},{7,15},{8,0},{9,1},... | collective-permute-start | bytes 786440 | tf_op jit(solution)/shard_map/ppermute | solution.py:30
  88.1 2.4 %collective-permute-done.13 = bf16[32,4096]{1,0:T(8,128)(2,1)S(1)} collective-permute-done((bf16[32,4096]{1,0:T(8,128)(2,1)S(1)}, bf16[32,4096]{1,0:T(8,128)(2,1)S(1)}, u32[]{:S(2)}, u32[]{:S(2)}) %collective-permute-start.13) | collective-permute-done | bytes 262176 | tf_op jit(solution)/shard_map/ppermute | solution.py:30
  90.5 9.2 %collective-permute-done.17 = bf16[32,4096]{1,0:T(8,128)(2,1)S(1)} collective-permute-done((bf16[32,4096]{1,0:T(8,128)(2,1)S(1)}, bf16[32,4096]{1,0:T(8,128)(2,1)S(1)}, u32[]{:S(2)}, u32[]{:S(2)}) %collective-permute-start.17) | collective-permute-done | bytes 262176 | tf_op jit(solution)/shard_map/ppermute | solution.py:30
  (23 shorter events, 9.1 us)
Async XLA Ops:
  0.6 45.2 %copy-start.1 = (bf16[2,1,48,16,128]{4,3,2,1,0:T(8,128)(2,1)S(1)}, bf16[2,1,48,16,128]{4,3,2,1,0:T(8,128)(2,1)}, u32[]{:S(2)}) copy-start(bf16[2,1,48,16,128]{4,3,2,1,0:T(8,128)(2,1)} %mine_ref.1) | copy-start | bytes 1179652
  0.6 48.4 %collective-permute-start.7 = (bf16[4096,384]{1,0:T(8,128)(2,1)}, bf16[4096,384]{1,0:T(8,128)(2,1)S(1)}, u32[]{:S(2)}, u32[]{:S(2)}) collective-permute-start(bf16[4096,384]{1,0:T(8,128)(2,1)} %refs_6_.1), channel_id=1, source_target_pairs={{0,1},{1,0},{2,3},{3,2},{4,5},{5,4},{6,7},{7,6},{8,9},{9,8},{10,11... | collective-permute-start | bytes 9437192 | tf_op jit(solution)/shard_map/ppermute | solution.py:30
  9.5 18.3 %collective-permute-start.3 = (bf16[32,4096]{1,0:T(8,128)(2,1)}, bf16[32,4096]{1,0:T(8,128)(2,1)S(1)}, u32[]{:S(2)}, u32[]{:S(2)}) collective-permute-start(bf16[32,4096]{1,0:T(8,128)(2,1)} %refs_5_.1), channel_id=1, source_target_pairs={{0,8},{1,9},{2,10},{3,11},{4,12},{5,13},{6,14},{7,15},{8,0},{9,1},... | collective-permute-start | bytes 786440 | tf_op jit(solution)/shard_map/ppermute | solution.py:30
  11.6 43.0 %collective-permute-start.10 = (bf16[128,4096]{1,0:T(8,128)(2,1)}, bf16[128,4096]{1,0:T(8,128)(2,1)S(1)}, u32[]{:S(2)}, u32[]{:S(2)}) collective-permute-start(bf16[128,4096]{1,0:T(8,128)(2,1)} %out_mine_ref.1), channel_id=1, source_target_pairs={{0,1},{1,0},{2,3},{3,2},{4,5},{5,4},{6,7},{7,6},{8,9},{9,8},{10,11... | collective-permute-start | bytes 3145736 | tf_op jit(solution)/shard_map/ppermute | solution.py:30
  13.9 15.9 %collective-permute-start = (bf16[32,4096]{1,0:T(8,128)(2,1)}, bf16[32,4096]{1,0:T(8,128)(2,1)S(1)}, u32[]{:S(2)}, u32[]{:S(2)}) collective-permute-start(bf16[32,4096]{1,0:T(8,128)(2,1)} %refs_5_.1), channel_id=1, source_target_pairs={{0,2},{1,3},{2,4},{3,5},{4,6},{5,7},{6,0},{7,1},{8,10},{9,11},{10,... | collective-permute-start | bytes 786440 | tf_op jit(solution)/shard_map/ppermute | solution.py:30
  17.0 16.1 %collective-permute-start.1 = (bf16[32,4096]{1,0:T(8,128)(2,1)}, bf16[32,4096]{1,0:T(8,128)(2,1)S(1)}, u32[]{:S(2)}, u32[]{:S(2)}) collective-permute-start(bf16[32,4096]{1,0:T(8,128)(2,1)} %refs_5_.1), channel_id=1, source_target_pairs={{0,4},{1,5},{2,6},{3,7},{4,0},{5,1},{6,2},{7,3},{8,12},{9,13},{10,... | collective-permute-start | bytes 786440 | tf_op jit(solution)/shard_map/ppermute | solution.py:30
  27.8 9.5 %collective-permute-start.2 = (bf16[32,4096]{1,0:T(8,128)(2,1)}, bf16[32,4096]{1,0:T(8,128)(2,1)S(1)}, u32[]{:S(2)}, u32[]{:S(2)}) collective-permute-start(bf16[32,4096]{1,0:T(8,128)(2,1)} %refs_5_.1), channel_id=1, source_target_pairs={{0,6},{1,7},{2,0},{3,1},{4,2},{5,3},{6,4},{7,5},{8,14},{9,15},{10,... | collective-permute-start | bytes 786440 | tf_op jit(solution)/shard_map/ppermute | solution.py:30
  29.7 16.1 %collective-permute-start.4 = (bf16[32,4096]{1,0:T(8,128)(2,1)S(1)}, bf16[32,4096]{1,0:T(8,128)(2,1)S(1)}, u32[]{:S(2)}, u32[]{:S(2)}) collective-permute-start(bf16[32,4096]{1,0:T(8,128)(2,1)S(1)} %collective-permute-done.3.refs_4_), channel_id=1, source_target_pairs={{0,2},{1,3},{2,4},{3,5},{4,6},{5,7},{6,0},{7,1},{8,10},{9,11},{10,... | collective-permute-start | bytes 786440 | tf_op jit(solution)/shard_map/ppermute | solution.py:30
  33.1 16.0 %collective-permute-start.5 = (bf16[32,4096]{1,0:T(8,128)(2,1)S(1)}, bf16[32,4096]{1,0:T(8,128)(2,1)S(1)}, u32[]{:S(2)}, u32[]{:S(2)}) collective-permute-start(bf16[32,4096]{1,0:T(8,128)(2,1)S(1)} %collective-permute-done.3.refs_4_), channel_id=1, source_target_pairs={{0,4},{1,5},{2,6},{3,7},{4,0},{5,1},{6,2},{7,3},{8,12},{9,13},{10,... | collective-permute-start | bytes 786440 | tf_op jit(solution)/shard_map/ppermute | solution.py:30
  37.3 11.8 %collective-permute-start.6 = (bf16[32,4096]{1,0:T(8,128)(2,1)S(1)}, bf16[32,4096]{1,0:T(8,128)(2,1)S(1)}, u32[]{:S(2)}, u32[]{:S(2)}) collective-permute-start(bf16[32,4096]{1,0:T(8,128)(2,1)S(1)} %collective-permute-done.3.refs_4_), channel_id=1, source_target_pairs={{0,6},{1,7},{2,0},{3,1},{4,2},{5,3},{6,4},{7,5},{8,14},{9,15},{10,... | collective-permute-start | bytes 786440 | tf_op jit(solution)/shard_map/ppermute | solution.py:30
  45.9 8.8 %collective-permute-start.9 = (bf16[2,1,48,16,128]{4,3,2,1,0:T(8,128)(2,1)S(1)}, bf16[2,1,48,16,128]{4,3,2,1,0:T(8,128)(2,1)S(1)}, u32[]{:S(2)}, u32[]{:S(2)}) collective-permute-start(bf16[2,1,48,16,128]{4,3,2,1,0:T(8,128)(2,1)S(1)} %copy-done.1), channel_id=1, source_target_pairs={{0,1},{1,0},{2,3},{3,2},{4,5},{5,4},{6,7},{7,6},{8,9},{9,8},{10,11... | collective-permute-start | bytes 1179656 | tf_op jit(solution)/shard_map/ppermute | solution.py:30
  49.1 6.7 %copy-start = (bf16[128,4096]{1,0:T(8,128)(2,1)S(1)}, bf16[128,4096]{1,0:T(8,128)(2,1)}, u32[]{:S(2)}) copy-start(bf16[128,4096]{1,0:T(8,128)(2,1)} %out_mine_ref.1) | copy-start | bytes 3145732
  52.0 3.8 %collective-permute-start.8 = (bf16[256,512]{1,0:T(8,128)(2,1)S(1)}, bf16[256,512]{1,0:T(8,128)(2,1)S(1)}, u32[]{:S(2)}, u32[]{:S(2)}) collective-permute-start(bf16[256,512]{1,0:T(8,128)(2,1)S(1)} %get-tuple-element.21.near_ref), channel_id=1, source_target_pairs={{0,1},{1,0},{2,3},{3,2},{4,5},{5,4},{6,7},{7,6},{8,9},{9,8},{10,11... | collective-permute-start | bytes 786440 | tf_op jit(solution)/shard_map/ppermute | solution.py:30
  58.7 16.3 %collective-permute-start.14 = (bf16[32,4096]{1,0:T(8,128)(2,1)S(1)}, bf16[32,4096]{1,0:T(8,128)(2,1)S(1)}, u32[]{:S(2)}, u32[]{:S(2)}) collective-permute-start(bf16[32,4096]{1,0:T(8,128)(2,1)S(1)} %get-tuple-element.28), channel_id=1, source_target_pairs={{0,6},{1,7},{2,0},{3,1},{4,2},{5,3},{6,4},{7,5},{8,14},{9,15},{10,... | collective-permute-start | bytes 786440 | tf_op jit(solution)/shard_map/ppermute | solution.py:30
  63.0 15.2 %collective-permute-start.15 = (bf16[32,4096]{1,0:T(8,128)(2,1)S(1)}, bf16[32,4096]{1,0:T(8,128)(2,1)S(1)}, u32[]{:S(2)}, u32[]{:S(2)}) collective-permute-start(bf16[32,4096]{1,0:T(8,128)(2,1)S(1)} %get-tuple-element.29), channel_id=1, source_target_pairs={{0,4},{1,5},{2,6},{3,7},{4,0},{5,1},{6,2},{7,3},{8,12},{9,13},{10,... | collective-permute-start | bytes 786440 | tf_op jit(solution)/shard_map/ppermute | solution.py:30
  65.3 14.9 %collective-permute-start.16 = (bf16[32,4096]{1,0:T(8,128)(2,1)S(1)}, bf16[32,4096]{1,0:T(8,128)(2,1)S(1)}, u32[]{:S(2)}, u32[]{:S(2)}) collective-permute-start(bf16[32,4096]{1,0:T(8,128)(2,1)S(1)} %get-tuple-element.30), channel_id=1, source_target_pairs={{0,2},{1,3},{2,4},{3,5},{4,6},{5,7},{6,0},{7,1},{8,10},{9,11},{10,... | collective-permute-start | bytes 786440 | tf_op jit(solution)/shard_map/ppermute | solution.py:30
  67.4 20.6 %collective-permute-start.11 = (bf16[32,4096]{1,0:T(8,128)(2,1)S(1)}, bf16[32,4096]{1,0:T(8,128)(2,1)S(1)}, u32[]{:S(2)}, u32[]{:S(2)}) collective-permute-start(bf16[32,4096]{1,0:T(8,128)(2,1)S(1)} %get-tuple-element.24), channel_id=1, source_target_pairs={{0,6},{1,7},{2,0},{3,1},{4,2},{5,3},{6,4},{7,5},{8,14},{9,15},{10,... | collective-permute-start | bytes 786440 | tf_op jit(solution)/shard_map/ppermute | solution.py:30
  71.8 16.2 %collective-permute-start.12 = (bf16[32,4096]{1,0:T(8,128)(2,1)S(1)}, bf16[32,4096]{1,0:T(8,128)(2,1)S(1)}, u32[]{:S(2)}, u32[]{:S(2)}) collective-permute-start(bf16[32,4096]{1,0:T(8,128)(2,1)S(1)} %get-tuple-element.25), channel_id=1, source_target_pairs={{0,2},{1,3},{2,4},{3,5},{4,6},{5,7},{6,0},{7,1},{8,10},{9,11},{10,... | collective-permute-start | bytes 786440 | tf_op jit(solution)/shard_map/ppermute | solution.py:30
  75.0 15.5 %collective-permute-start.13 = (bf16[32,4096]{1,0:T(8,128)(2,1)S(1)}, bf16[32,4096]{1,0:T(8,128)(2,1)S(1)}, u32[]{:S(2)}, u32[]{:S(2)}) collective-permute-start(bf16[32,4096]{1,0:T(8,128)(2,1)S(1)} %get-tuple-element.26), channel_id=1, source_target_pairs={{0,4},{1,5},{2,6},{3,7},{4,0},{5,1},{6,2},{7,3},{8,12},{9,13},{10,... | collective-permute-start | bytes 786440 | tf_op jit(solution)/shard_map/ppermute | solution.py:30
  80.4 19.4 %collective-permute-start.17 = (bf16[32,4096]{1,0:T(8,128)(2,1)S(1)}, bf16[32,4096]{1,0:T(8,128)(2,1)S(1)}, u32[]{:S(2)}, u32[]{:S(2)}) collective-permute-start(bf16[32,4096]{1,0:T(8,128)(2,1)S(1)} %add_convert_fusion.1), channel_id=1, source_target_pairs={{0,8},{1,9},{2,10},{3,11},{4,12},{5,13},{6,14},{7,15},{8,0},{9,1},... | collective-permute-start | bytes 786440 | tf_op jit(solution)/shard_map/ppermute | solution.py:30

commit v3 on v2

--- a/solution.py
+++ b/solution.py
@@ -1,3 +1,5 @@
+import functools
+
 import jax
 import jax.numpy as jnp
 from jax import lax
@@ -28,6 +30,11 @@
         for c in range(2)
     ]
     return lax.ppermute(value, "tp", pairs)
+
+
+def along_x(value):
+    groups = [[tp_of(y, x, c) for x in range(N_X)] for y in range(2) for c in range(2)]
+    return lax.all_to_all(value, "tp", 0, 0, axis_index_groups=groups)
 
 
 def my_place():
@@ -141,7 +148,7 @@
 
 
 def project_kernel(*refs):
-    pieces, (gain_ref, mine_ref, other_ref, q_ref, kv_ref, normed) = refs[:8], refs[8:]
+    pieces, (gain_ref, mine_ref, other_ref, normed, kv_ref) = refs[:8], refs[8:]
     gain = jnp.concatenate([gain_ref[k : k + 1, :] for k in range(gain_ref.shape[0])], axis=1)
     gain = gain.astype(jnp.float32)
     for i, ref in enumerate(pieces):
@@ -157,13 +164,13 @@
     def times(right):
         return jnp.dot(left, right, preferred_element_type=jnp.float32).astype(jnp.bfloat16)
 
-    first = times(mine_ref[:, :256])
-    q_ref[:, :128] = first[:, :128]
-    kv_ref[:, :128] = first[:, 128:]
-    middle = times(jnp.concatenate([mine_ref[:, 256:], other_ref[:, :128]], axis=1))
-    kv_ref[:, 128:256] = middle[:, :128]
-    q_ref[:, 128:] = middle[:, 128:]
+    kv_ref[:, :256] = times(mine_ref[:, 128:])
     kv_ref[:, 256:] = times(other_ref[:, 128:])
+
+
+def query_kernel(normed, mine_ref, other_ref, q_ref):
+    both = jnp.concatenate([mine_ref[:, :128], other_ref[:, :128]], axis=1)
+    q_ref[...] = jnp.dot(normed[...], both, preferred_element_type=jnp.float32).astype(jnp.bfloat16)
 
 
 def project(pieces, gain, mine, other):
@@ -171,18 +178,32 @@
     return pl.pallas_call(
         project_kernel,
         out_shape=(
-            jax.ShapeDtypeStruct((256, 256), jnp.bfloat16),
+            jax.ShapeDtypeStruct((256, 4096), jnp.bfloat16),
             jax.ShapeDtypeStruct((256, 512), jnp.bfloat16),
         ),
         in_specs=[vmem] * 11,
         out_specs=(vmem, vmem),
-        scratch_shapes=[pltpu.VMEM((256, 4096), jnp.bfloat16)],
         compiler_params=pltpu.CompilerParams(vmem_limit_bytes=24 * 2**20),
         cost_estimate=pl.CostEstimate(
-            flops=2 * 256 * 4096 * 768, bytes_accessed=9_000_000, transcendentals=0
+            flops=2 * 256 * 4096 * 512, bytes_accessed=9_000_000, transcendentals=0
         ),
         name="project",
     )(*[in_vmem(piece) for piece in pieces], in_vmem(gain), in_vmem(mine), in_vmem(other))
+
+
+def query(normed, mine, other):
+    vmem = pl.BlockSpec(memory_space=pltpu.VMEM)
+    return pl.pallas_call(
+        query_kernel,
+        out_shape=jax.ShapeDtypeStruct((256, 256), jnp.bfloat16),
+        in_specs=[vmem] * 3,
+        out_specs=vmem,
+        compiler_params=pltpu.CompilerParams(vmem_limit_bytes=24 * 2**20),
+        cost_estimate=pl.CostEstimate(
+            flops=2 * 256 * 4096 * 256, bytes_accessed=5_000_000, transcendentals=0
+        ),
+        name="query",
+    )(in_vmem(normed), in_vmem(mine), in_vmem(other))
 
 
 def out_rows(left, right, mine_ref, other_ref, out_refs):
@@ -192,14 +213,20 @@
             jnp.dot(left, mine_ref[:, lanes], preferred_element_type=jnp.float32)
             + jnp.dot(right, other_ref[:, lanes], preferred_element_type=jnp.float32)
         ).astype(jnp.bfloat16)
-        for i, out_ref in enumerate(out_refs):
-            out_ref[:, lanes] = partial[i * BLOCK : (i + 1) * BLOCK]
+        for i in range(N_X):
+            rows = partial[i * BLOCK : (i + 1) * BLOCK]
+            if len(out_refs) == 1:
+                x = my_place()[1]
+                out_refs[0][(x - i) & 3, :, lanes] = rows
+            else:
+                out_refs[i][:, lanes] = rows
 
 
 def attend_kernel(
-    q_ref, near_ref, mine_ref, dist_ref, away_ref, other_ref, out_mine_ref, out_other_ref, *rest,
+    half, q_ref, near_ref, mine_ref, dist_ref, away_ref, other_ref, out_mine_ref, out_other_ref, *rest,
 ):
-    out_refs, (scores, weights, context_ref) = rest[:8], rest[8:]
+    out_refs, (scores, weights, context_ref) = rest[:-3], rest[-3:]
+    mine_rows = slice(half * 128, half * 128 + 128)
     y, x, c = my_place()
     cached = (mine_ref, other_ref)
     turned = (((1,), (1,)), ((), ()))
@@ -210,7 +237,7 @@
         slope = log2e * jnp.exp2(
             jnp.full((1, 128), -8.0 * (MODEL_HEADS // N_TP) / MODEL_HEADS, jnp.float32) * at
         )
-        q = q_ref[:, columns]
+        q = q_ref[mine_rows, columns]
         new = ((near_ref, head * 256), (away_ref, (1 - head) * 256))
         scores[:, :768] = lax.dot_general(
             q, cached[head][0, 0].reshape(768, HEAD), turned, preferred_element_type=jnp.float32
@@ -220,13 +247,14 @@
                 q, ref[:, first : first + HEAD], turned, preferred_element_type=jnp.float32
             )
         sums = []
-        for b in range(8):
+        for b in range(N_X):
             rows = slice(b * BLOCK, (b + 1) * BLOCK)
+            table = slice(half * 128 + b * BLOCK, half * 128 + (b + 1) * BLOCK)
             pieces = []
             peak = None
             for k in range(10):
                 lanes = slice(k * 128, (k + 1) * 128)
-                piece = scores[rows, lanes] * (log2e * HEAD ** (-0.5)) - slope * dist_ref[rows, lanes]
+                piece = scores[rows, lanes] * (log2e * HEAD ** (-0.5)) - slope * dist_ref[table, lanes]
                 peak = piece if peak is None else jnp.maximum(peak, piece)
                 pieces.append(piece)
             peak = jnp.max(peak, axis=1, keepdims=True)
@@ -245,34 +273,36 @@
                 ref[:, first + HEAD : first + 2 * HEAD],
                 preferred_element_type=jnp.float32,
             )
-        for b in range(8):
+        for b in range(N_X):
             context_ref[b * BLOCK : (b + 1) * BLOCK, columns] = (
                 result[b * BLOCK : (b + 1) * BLOCK] / sums[b]
             ).astype(jnp.bfloat16)
     out_rows(context_ref[:, :HEAD], context_ref[:, HEAD:], out_mine_ref, out_other_ref, out_refs)
 
 
-def attend(queries, near, away, mine, other, dist, out_mine, out_other):
+def attend(half, operands):
     vmem = pl.BlockSpec(memory_space=pltpu.VMEM)
-    operands = (queries, near, mine, dist, away, other, out_mine, out_other)
+    shapes = [jax.ShapeDtypeStruct((BLOCK, 4096), jnp.bfloat16)] * N_X
+    if half == 0:
+        shapes = [jax.ShapeDtypeStruct((N_X, BLOCK, 4096), jnp.bfloat16)]
     return pl.pallas_call(
-        attend_kernel,
-        out_shape=[jax.ShapeDtypeStruct((BLOCK, 4096), jnp.bfloat16)] * 8,
+        functools.partial(attend_kernel, half),
+        out_shape=shapes,
         in_specs=[vmem] * 8,
-        out_specs=[vmem] * 8,
+        out_specs=[vmem] * len(shapes),
         scratch_shapes=[
-            pltpu.VMEM((256, 1280), jnp.float32),
-            pltpu.VMEM((256, 1280), jnp.bfloat16),
-            pltpu.VMEM((256, 256), jnp.bfloat16),
+            pltpu.VMEM((128, 1280), jnp.float32),
+            pltpu.VMEM((128, 1280), jnp.bfloat16),
+            pltpu.VMEM((128, 256), jnp.bfloat16),
         ],
         compiler_params=pltpu.CompilerParams(vmem_limit_bytes=24 * 2**20),
         cost_estimate=pl.CostEstimate(
-            flops=4 * 256 * 1280 * 256 + 2 * 256 * 256 * 4096,
-            bytes_accessed=8_000_000,
-            transcendentals=2 * 256 * 1280,
+            flops=4 * 128 * 1280 * 256 + 2 * 128 * 256 * 4096,
+            bytes_accessed=6_000_000,
+            transcendentals=2 * 128 * 1280,
         ),
         name="attend",
-    )(*[in_vmem(operand) for operand in operands])
+    )(*operands)
 
 
 def fresh_kernel(target_ref, near_ref, away_ref, out_ref):
@@ -333,21 +363,22 @@
         segment_ids, prefix_pages, page_order, fresh_order,
         norm_gain.reshape(32, 128), tokens, qkv_weight,
     )
-    queries, near = project(own + across, gain, qkv_mine, qkv_other)
+    normed, near = project(own + across, gain, qkv_mine, qkv_other)
     away = moved(near, 0, 0, 1)
-    partial = attend(queries, near, away, cache_pool, cache_other, dist, out_weight, out_other)
-    kept, passed = partial[:4], partial[4:]
+    queries = query(normed, qkv_mine, qkv_other)
+    operands = (queries, near, cache_pool, dist, away, cache_other, out_weight, out_other)
+    operands = tuple(in_vmem(operand) for operand in operands)
+    passed = attend(1, operands)
+    kept = attend(0, operands)
     passed_in = [passed[0]]
     for dx in (1, 2, 3):
         passed_in.append(moved(passed[dx], 0, -dx, 0))
-    kept_in = [kept[0]]
-    for dx in (1, 2, 3):
-        kept_in.append(moved(kept[dx], 0, -dx, 0))
+    kept_in = along_x(kept[0])
     passed_sum = added(passed_in).astype(jnp.bfloat16)
     from_partner = moved(passed_sum, 1, 0, 0)
     fresh_pages = fresh(target, near, away, fresh_order.shape[0])
-    kept_sum = lax.optimization_barrier(added([kept_in[0], kept_in[1], kept_in[3]]))
-    summed = added([kept_sum, kept_in[2], from_partner]).astype(jnp.bfloat16)
+    kept_sum = lax.optimization_barrier(jnp.sum(kept_in.astype(jnp.float32), axis=0))
+    summed = added([kept_sum, from_partner]).astype(jnp.bfloat16)
     return (summed, fresh_pages.reshape(2, 1, fresh_order.shape[0], PAGE, HEAD))
 
 

time: 101 us -> 99.7 us (0.987)
  starting transfers between devices: 63 us -> 55.9 us
  waiting for transfers between devices: 26.6 us -> 30.1 us
  Pallas kernels: 9.07 us -> 11.1 us
    ppermute x18 -> x15, starting transfers between devices: 63 us -> 51.1 us  [moved(): return lax.ppermute(value, 'tp', pairs)]
    all_to_all x0 -> x1, starting transfers between devices: none -> 4.83 us  [along_x(): return lax.all_to_all(value, 'tp', 0, 0, axis_index_groups=groups)]
    ppermute x18 -> x15, waiting for transfers between devices: 26.6 us -> 28.7 us  [moved(): return lax.ppermute(value, 'tp', pairs)]
    pallas_call x2 -> x4, Pallas kernels: 5.79 us -> 7.82 us  [the longest x2 4.54 us: attend(): pl.pallas_call(functools.partial(attend_kernel, half), out_shape=shapes,...]
    all_to_all x0 -> x1, waiting for transfers between devices: none -> 1.41 us  [along_x(): return lax.all_to_all(value, 'tp', 0, 0, axis_index_groups=groups)]
  transfers between devices with their start and end apart: 18 -> 16, of which waited for: 7 -> 7; matrix products, arithmetic and copies ran while one was open for 0% -> 0% of each run, Pallas kernels for 6% -> 9%
where the time goes in v3:
time: 99.7 us; the launch traced here: 99 us
  starting transfers between devices  55.9 us (56%)
  waiting for transfers between devices  30.1 us (30%)
  Pallas kernels  11.1 us (11%)
  other arithmetic  1.04 us (1%)
    ppermute x15, starting transfers between devices, moved(): return lax.ppermute(value, 'tp', pairs)  51.1 us
    ppermute x15, waiting for transfers between devices, moved(): return lax.ppermute(value, 'tp', pairs)  28.7 us
    all_to_all x1, starting transfers between devices, along_x(): return lax.all_to_all(value, 'tp', 0, 0, axis_index_groups=groups)  4.83 us
    pallas_call x2, Pallas kernels, attend(): pl.pallas_call(functools.partial(attend_kernel, half), out_shape=shapes,...  4.54 us
    pallas_call x1, Pallas kernels, project(): pl.pallas_call(project_kernel, out_shape=(jax.ShapeDtypeStruct((256, 4096...  2.52 us
    pallas_call x1, Pallas kernels, layout_tables(): pl.pallas_call(layout_kernel, out_shape=[jax.ShapeDtypeStruct((256, 1280)...  2.08 us
  transfers between devices with their start and end apart: 16, of which 7 were waited for; matrix products, arithmetic and copies ran while one was open for 0% of the time, Pallas kernels for 9%

profile of v3, /device:TPU:1, one launch (start us, length us, event | category | flops | bytes accessed | tf_op | source)
XLA Modules:
  0.0 99.0 jit_solution(7743317579900801993)
XLA Ops:
  0.6 8.7 %collective-permute-start.7 = (bf16[4096,384]{1,0:T(8,128)(2,1)}, bf16[4096,384]{1,0:T(8,128)(2,1)S(1)}, u32[]{:S(2)}, u32[]{:S(2)}) collective-permute-start(bf16[4096,384]{1,0:T(8,128)(2,1)} %refs_6_.1), channel_id=1, source_target_pairs={{0,1},{1,0},{2,3},{3,2},{4,5},{5,4},{6,7},{7,6},{8,9},{9,8},{10,11... | collective-permute-start | bytes 9437192 | tf_op jit(solution)/shard_map/ppermute | solution.py:32
  9.4 2.1 %collective-permute-start.3 = (bf16[32,4096]{1,0:T(8,128)(2,1)}, bf16[32,4096]{1,0:T(8,128)(2,1)S(1)}, u32[]{:S(2)}, u32[]{:S(2)}) collective-permute-start(bf16[32,4096]{1,0:T(8,128)(2,1)} %refs_5_.1), channel_id=1, source_target_pairs={{0,8},{1,9},{2,10},{3,11},{4,12},{5,13},{6,14},{7,15},{8,0},{9,1},... | collective-permute-start | bytes 786440 | tf_op jit(solution)/shard_map/ppermute | solution.py:32
  11.5 2.2 %collective-permute-start.10 = (bf16[128,4096]{1,0:T(8,128)(2,1)}, bf16[128,4096]{1,0:T(8,128)(2,1)S(1)}, u32[]{:S(2)}, u32[]{:S(2)}) collective-permute-start(bf16[128,4096]{1,0:T(8,128)(2,1)} %out_mine_ref.3), channel_id=1, source_target_pairs={{0,1},{1,0},{2,3},{3,2},{4,5},{5,4},{6,7},{7,6},{8,9},{9,8},{10,11... | collective-permute-start | bytes 3145736 | tf_op jit(solution)/shard_map/ppermute | solution.py:32
  13.7 3.1 %collective-permute-start = (bf16[32,4096]{1,0:T(8,128)(2,1)}, bf16[32,4096]{1,0:T(8,128)(2,1)S(1)}, u32[]{:S(2)}, u32[]{:S(2)}) collective-permute-start(bf16[32,4096]{1,0:T(8,128)(2,1)} %refs_5_.1), channel_id=1, source_target_pairs={{0,2},{1,3},{2,4},{3,5},{4,6},{5,7},{6,0},{7,1},{8,10},{9,11},{10,... | collective-permute-start | bytes 786440 | tf_op jit(solution)/shard_map/ppermute | solution.py:32
  16.8 4.4 %collective-permute-start.1 = (bf16[32,4096]{1,0:T(8,128)(2,1)}, bf16[32,4096]{1,0:T(8,128)(2,1)S(1)}, u32[]{:S(2)}, u32[]{:S(2)}) collective-permute-start(bf16[32,4096]{1,0:T(8,128)(2,1)} %refs_5_.1), channel_id=1, source_target_pairs={{0,4},{1,5},{2,6},{3,7},{4,0},{5,1},{6,2},{7,3},{8,12},{9,13},{10,... | collective-permute-start | bytes 786440 | tf_op jit(solution)/shard_map/ppermute | solution.py:32
  21.2 6.4 %collective-permute-done.3.refs_4_ = bf16[32,4096]{1,0:T(8,128)(2,1)S(1)} collective-permute-done((bf16[32,4096]{1,0:T(8,128)(2,1)}, bf16[32,4096]{1,0:T(8,128)(2,1)S(1)}, u32[]{:S(2)}, u32[]{:S(2)}) %collective-permute-start.3) | collective-permute-done | bytes 262176 | tf_op jit(solution)/shard_map/ppermute | solution.py:32
  27.6 1.9 %collective-permute-start.2 = (bf16[32,4096]{1,0:T(8,128)(2,1)}, bf16[32,4096]{1,0:T(8,128)(2,1)S(1)}, u32[]{:S(2)}, u32[]{:S(2)}) collective-permute-start(bf16[32,4096]{1,0:T(8,128)(2,1)} %refs_5_.1), channel_id=1, source_target_pairs={{0,6},{1,7},{2,0},{3,1},{4,2},{5,3},{6,4},{7,5},{8,14},{9,15},{10,... | collective-permute-start | bytes 786440 | tf_op jit(solution)/shard_map/ppermute | solution.py:32
  29.6 3.4 %collective-permute-start.4 = (bf16[32,4096]{1,0:T(8,128)(2,1)S(1)}, bf16[32,4096]{1,0:T(8,128)(2,1)S(1)}, u32[]{:S(2)}, u32[]{:S(2)}) collective-permute-start(bf16[32,4096]{1,0:T(8,128)(2,1)S(1)} %collective-permute-done.3.refs_4_), channel_id=1, source_target_pairs={{0,2},{1,3},{2,4},{3,5},{4,6},{5,7},{6,0},{7,1},{8,10},{9,11},{10,... | collective-permute-start | bytes 786440 | tf_op jit(solution)/shard_map/ppermute | solution.py:32
  33.0 1.9 %collective-permute-start.5 = (bf16[32,4096]{1,0:T(8,128)(2,1)S(1)}, bf16[32,4096]{1,0:T(8,128)(2,1)S(1)}, u32[]{:S(2)}, u32[]{:S(2)}) collective-permute-start(bf16[32,4096]{1,0:T(8,128)(2,1)S(1)} %collective-permute-done.3.refs_4_), channel_id=1, source_target_pairs={{0,4},{1,5},{2,6},{3,7},{4,0},{5,1},{6,2},{7,3},{8,12},{9,13},{10,... | collective-permute-start | bytes 786440 | tf_op jit(solution)/shard_map/ppermute | solution.py:32
  34.9 2.3 %collective-permute-done.2.refs_3_ = bf16[32,4096]{1,0:T(8,128)(2,1)S(1)} collective-permute-done((bf16[32,4096]{1,0:T(8,128)(2,1)}, bf16[32,4096]{1,0:T(8,128)(2,1)S(1)}, u32[]{:S(2)}, u32[]{:S(2)}) %collective-permute-start.2) | collective-permute-done | bytes 262176 | tf_op jit(solution)/shard_map/ppermute | solution.py:32
  37.2 3.4 %collective-permute-start.6 = (bf16[32,4096]{1,0:T(8,128)(2,1)S(1)}, bf16[32,4096]{1,0:T(8,128)(2,1)S(1)}, u32[]{:S(2)}, u32[]{:S(2)}) collective-permute-start(bf16[32,4096]{1,0:T(8,128)(2,1)S(1)} %collective-permute-done.3.refs_4_), channel_id=1, source_target_pairs={{0,6},{1,7},{2,0},{3,1},{4,2},{5,3},{6,4},{7,5},{8,14},{9,15},{10,... | collective-permute-start | bytes 786440 | tf_op jit(solution)/shard_map/ppermute | solution.py:32
  40.6 5.1 %collective-permute-done.4.refs_5_ = bf16[32,4096]{1,0:T(8,128)(2,1)S(1)} collective-permute-done((bf16[32,4096]{1,0:T(8,128)(2,1)S(1)}, bf16[32,4096]{1,0:T(8,128)(2,1)S(1)}, u32[]{:S(2)}, u32[]{:S(2)}) %collective-permute-start.4) | collective-permute-done | bytes 262176 | tf_op jit(solution)/shard_map/ppermute | solution.py:32
  45.7 3.2 %collective-permute-start.9 = (bf16[2,1,48,16,128]{4,3,2,1,0:T(8,128)(2,1)}, bf16[2,1,48,16,128]{4,3,2,1,0:T(8,128)(2,1)S(1)}, u32[]{:S(2)}, u32[]{:S(2)}) collective-permute-start(bf16[2,1,48,16,128]{4,3,2,1,0:T(8,128)(2,1)} %mine_ref.3), channel_id=1, source_target_pairs={{0,1},{1,0},{2,3},{3,2},{4,5},{5,4},{6,7},{7,6},{8,9},{9,8},{10,11... | collective-permute-start | bytes 1179656 | tf_op jit(solution)/shard_map/ppermute | solution.py:32
  48.9 2.1 %layout.1 = (f32[256,1280]{1,0:T(8,128)S(1)}, s32[8,128]{1,0:T(8,128)S(1)}, bf16[32,128]{1,0:T(8,128)(2,1)S(1)}, bf16[32,4096]{1,0:T(8,128)(2,1)S(1)}, bf16[4096,384]{1,0:T(8,128)(2,1)S(1)}) custom-call(s32[4,128]{1,0:T(4,128)} %bitcast.7, s32[8]{0:T(128)} %refs_1_.1, s32[48]{0:T(128)} %refs_2_.1, s32[40]{0:T(128)} %refs_3_.1, bf16[32,128]{1,0:T(8,128)(2,1)} %bitcast.6, ...), custom_call_target="tpu_custom_call" | custom-call | bytes 6000000 | tf_op jit(solution)/shard_map/layout/pallas_call | solution.py:132
  51.0 2.5 %project.1 = (bf16[256,4096]{1,0:T(8,128)(2,1)S(1)}, bf16[256,512]{1,0:T(8,128)(2,1)S(1)}) custom-call(bf16[32,4096]{1,0:T(8,128)(2,1)S(1)} %get-tuple-element.13.refs_0_, bf16[32,4096]{1,0:T(8,128)(2,1)S(1)} %collective-permute-done.refs_1_, bf16[32,4096]{1,0:T(8,128)(2,1)S(1)} %collective-permute-done.1.refs_2_, ...), custom_call_target="tpu_custom_call" | custom-call | flops 1073741824 | bytes 9000000 | tf_op jit(solution)/shard_map/project/pallas_call | solution.py:178
  53.6 1.9 %collective-permute-start.8 = (bf16[256,512]{1,0:T(8,128)(2,1)S(1)}, bf16[256,512]{1,0:T(8,128)(2,1)S(1)}, u32[]{:S(2)}, u32[]{:S(2)}) collective-permute-start(bf16[256,512]{1,0:T(8,128)(2,1)S(1)} %get-tuple-element.17.near_ref), channel_id=1, source_target_pairs={{0,1},{1,0},{2,3},{3,2},{4,5},{5,4},{6,7},{7,6},{8,9},{9,8},{10,11... | collective-permute-start | bytes 786440 | tf_op jit(solution)/shard_map/ppermute | solution.py:32
  58.8 2.8 %collective-permute-start.11 = (bf16[32,4096]{1,0:T(8,128)(2,1)S(1)}, bf16[32,4096]{1,0:T(8,128)(2,1)S(1)}, u32[]{:S(2)}, u32[]{:S(2)}) collective-permute-start(bf16[32,4096]{1,0:T(8,128)(2,1)S(1)} %get-tuple-element.20), channel_id=1, source_target_pairs={{0,6},{1,7},{2,0},{3,1},{4,2},{5,3},{6,4},{7,5},{8,14},{9,15},{10,... | collective-permute-start | bytes 786440 | tf_op jit(solution)/shard_map/ppermute | solution.py:32
  61.5 2.3 %collective-permute-start.12 = (bf16[32,4096]{1,0:T(8,128)(2,1)S(1)}, bf16[32,4096]{1,0:T(8,128)(2,1)S(1)}, u32[]{:S(2)}, u32[]{:S(2)}) collective-permute-start(bf16[32,4096]{1,0:T(8,128)(2,1)S(1)} %get-tuple-element.21), channel_id=1, source_target_pairs={{0,4},{1,5},{2,6},{3,7},{4,0},{5,1},{6,2},{7,3},{8,12},{9,13},{10,... | collective-permute-start | bytes 786440 | tf_op jit(solution)/shard_map/ppermute | solution.py:32
  63.9 2.1 %collective-permute-start.13 = (bf16[32,4096]{1,0:T(8,128)(2,1)S(1)}, bf16[32,4096]{1,0:T(8,128)(2,1)S(1)}, u32[]{:S(2)}, u32[]{:S(2)}) collective-permute-start(bf16[32,4096]{1,0:T(8,128)(2,1)S(1)} %get-tuple-element.22), channel_id=1, source_target_pairs={{0,2},{1,3},{2,4},{3,5},{4,6},{5,7},{6,0},{7,1},{8,10},{9,11},{10,... | collective-permute-start | bytes 786440 | tf_op jit(solution)/shard_map/ppermute | solution.py:32
  66.0 2.8 %attend.2 = bf16[4,32,4096]{2,1,0:T(8,128)(2,1)} custom-call(bf16[256,256]{1,0:T(8,128)(2,1)S(1)} %query.1.q_ref, bf16[256,512]{1,0:T(8,128)(2,1)S(1)} %get-tuple-element.17.near_ref, bf16[2,1,48,16,128]{4,3,2,1,0:T(8,128)(2,1)S(1)} %copy-done.1, f32[256,1280]{1,0:T(8,128)S(1)} %get-tuple-element.18.dist_ref, ...), custom_call_target="tpu_custom_call" | custom-call | flops 436207616 | bytes 6000000 | tf_op jit(solution)/shard_map/attend/pallas_call | solution.py:288
  68.8 4.8 %all-to-all-start = ((bf16[4,32,4096]{2,1,0:T(8,128)(2,1)}), bf16[4,32,4096]{2,1,0:T(8,128)(2,1)S(1)}, u32[]{:S(2)}, u32[]{:S(2)}) async-start(bf16[4,32,4096]{2,1,0:T(8,128)(2,1)} %attend.2), calls=%async_computation | async-start | bytes 2097152 | tf_op jit(solution)/shard_map/all_to_all | solution.py:37
  73.6 5.2 %collective-permute-done.13 = bf16[32,4096]{1,0:T(8,128)(2,1)S(1)} collective-permute-done((bf16[32,4096]{1,0:T(8,128)(2,1)S(1)}, bf16[32,4096]{1,0:T(8,128)(2,1)S(1)}, u32[]{:S(2)}, u32[]{:S(2)}) %collective-permute-start.13) | collective-permute-done | bytes 262176 | tf_op jit(solution)/shard_map/ppermute | solution.py:32
  78.9 7.6 %collective-permute-start.14 = (bf16[32,4096]{1,0:T(8,128)(2,1)S(1)}, bf16[32,4096]{1,0:T(8,128)(2,1)S(1)}, u32[]{:S(2)}, u32[]{:S(2)}) collective-permute-start(bf16[32,4096]{1,0:T(8,128)(2,1)S(1)} %add_convert_fusion.1), channel_id=1, source_target_pairs={{0,8},{1,9},{2,10},{3,11},{4,12},{5,13},{6,14},{7,15},{8,0},{9,1},... | collective-permute-start | bytes 786440 | tf_op jit(solution)/shard_map/ppermute | solution.py:32
  89.4 8.9 %collective-permute-done.14 = bf16[32,4096]{1,0:T(8,128)(2,1)S(1)} collective-permute-done((bf16[32,4096]{1,0:T(8,128)(2,1)S(1)}, bf16[32,4096]{1,0:T(8,128)(2,1)S(1)}, u32[]{:S(2)}, u32[]{:S(2)}) %collective-permute-start.14) | collective-permute-done | bytes 262176 | tf_op jit(solution)/shard_map/ppermute | solution.py:32
  (21 shorter events, 6.9 us)
Async XLA Ops:
  0.6 50.4 %collective-permute-start.7 = (bf16[4096,384]{1,0:T(8,128)(2,1)}, bf16[4096,384]{1,0:T(8,128)(2,1)S(1)}, u32[]{:S(2)}, u32[]{:S(2)}) collective-permute-start(bf16[4096,384]{1,0:T(8,128)(2,1)} %refs_6_.1), channel_id=1, source_target_pairs={{0,1},{1,0},{2,3},{3,2},{4,5},{5,4},{6,7},{7,6},{8,9},{9,8},{10,11... | collective-permute-start | bytes 9437192 | tf_op jit(solution)/shard_map/ppermute | solution.py:32
  9.4 18.3 %collective-permute-start.3 = (bf16[32,4096]{1,0:T(8,128)(2,1)}, bf16[32,4096]{1,0:T(8,128)(2,1)S(1)}, u32[]{:S(2)}, u32[]{:S(2)}) collective-permute-start(bf16[32,4096]{1,0:T(8,128)(2,1)} %refs_5_.1), channel_id=1, source_target_pairs={{0,8},{1,9},{2,10},{3,11},{4,12},{5,13},{6,14},{7,15},{8,0},{9,1},... | collective-permute-start | bytes 786440 | tf_op jit(solution)/shard_map/ppermute | solution.py:32
  11.5 44.8 %collective-permute-start.10 = (bf16[128,4096]{1,0:T(8,128)(2,1)}, bf16[128,4096]{1,0:T(8,128)(2,1)S(1)}, u32[]{:S(2)}, u32[]{:S(2)}) collective-permute-start(bf16[128,4096]{1,0:T(8,128)(2,1)} %out_mine_ref.3), channel_id=1, source_target_pairs={{0,1},{1,0},{2,3},{3,2},{4,5},{5,4},{6,7},{7,6},{8,9},{9,8},{10,11... | collective-permute-start | bytes 3145736 | tf_op jit(solution)/shard_map/ppermute | solution.py:32
  13.7 15.9 %collective-permute-start = (bf16[32,4096]{1,0:T(8,128)(2,1)}, bf16[32,4096]{1,0:T(8,128)(2,1)S(1)}, u32[]{:S(2)}, u32[]{:S(2)}) collective-permute-start(bf16[32,4096]{1,0:T(8,128)(2,1)} %refs_5_.1), channel_id=1, source_target_pairs={{0,2},{1,3},{2,4},{3,5},{4,6},{5,7},{6,0},{7,1},{8,10},{9,11},{10,... | collective-permute-start | bytes 786440 | tf_op jit(solution)/shard_map/ppermute | solution.py:32
  16.8 16.1 %collective-permute-start.1 = (bf16[32,4096]{1,0:T(8,128)(2,1)}, bf16[32,4096]{1,0:T(8,128)(2,1)S(1)}, u32[]{:S(2)}, u32[]{:S(2)}) collective-permute-start(bf16[32,4096]{1,0:T(8,128)(2,1)} %refs_5_.1), channel_id=1, source_target_pairs={{0,4},{1,5},{2,6},{3,7},{4,0},{5,1},{6,2},{7,3},{8,12},{9,13},{10,... | collective-permute-start | bytes 786440 | tf_op jit(solution)/shard_map/ppermute | solution.py:32
  27.6 9.5 %collective-permute-start.2 = (bf16[32,4096]{1,0:T(8,128)(2,1)}, bf16[32,4096]{1,0:T(8,128)(2,1)S(1)}, u32[]{:S(2)}, u32[]{:S(2)}) collective-permute-start(bf16[32,4096]{1,0:T(8,128)(2,1)} %refs_5_.1), channel_id=1, source_target_pairs={{0,6},{1,7},{2,0},{3,1},{4,2},{5,3},{6,4},{7,5},{8,14},{9,15},{10,... | collective-permute-start | bytes 786440 | tf_op jit(solution)/shard_map/ppermute | solution.py:32
  29.6 16.1 %collective-permute-start.4 = (bf16[32,4096]{1,0:T(8,128)(2,1)S(1)}, bf16[32,4096]{1,0:T(8,128)(2,1)S(1)}, u32[]{:S(2)}, u32[]{:S(2)}) collective-permute-start(bf16[32,4096]{1,0:T(8,128)(2,1)S(1)} %collective-permute-done.3.refs_4_), channel_id=1, source_target_pairs={{0,2},{1,3},{2,4},{3,5},{4,6},{5,7},{6,0},{7,1},{8,10},{9,11},{10,... | collective-permute-start | bytes 786440 | tf_op jit(solution)/shard_map/ppermute | solution.py:32
  33.0 18.1 %collective-permute-start.5 = (bf16[32,4096]{1,0:T(8,128)(2,1)S(1)}, bf16[32,4096]{1,0:T(8,128)(2,1)S(1)}, u32[]{:S(2)}, u32[]{:S(2)}) collective-permute-start(bf16[32,4096]{1,0:T(8,128)(2,1)S(1)} %collective-permute-done.3.refs_4_), channel_id=1, source_target_pairs={{0,4},{1,5},{2,6},{3,7},{4,0},{5,1},{6,2},{7,3},{8,12},{9,13},{10,... | collective-permute-start | bytes 786440 | tf_op jit(solution)/shard_map/ppermute | solution.py:32
  37.2 13.9 %collective-permute-start.6 = (bf16[32,4096]{1,0:T(8,128)(2,1)S(1)}, bf16[32,4096]{1,0:T(8,128)(2,1)S(1)}, u32[]{:S(2)}, u32[]{:S(2)}) collective-permute-start(bf16[32,4096]{1,0:T(8,128)(2,1)S(1)} %collective-permute-done.3.refs_4_), channel_id=1, source_target_pairs={{0,6},{1,7},{2,0},{3,1},{4,2},{5,3},{6,4},{7,5},{8,14},{9,15},{10,... | collective-permute-start | bytes 786440 | tf_op jit(solution)/shard_map/ppermute | solution.py:32
  45.7 10.6 %collective-permute-start.9 = (bf16[2,1,48,16,128]{4,3,2,1,0:T(8,128)(2,1)}, bf16[2,1,48,16,128]{4,3,2,1,0:T(8,128)(2,1)S(1)}, u32[]{:S(2)}, u32[]{:S(2)}) collective-permute-start(bf16[2,1,48,16,128]{4,3,2,1,0:T(8,128)(2,1)} %mine_ref.3), channel_id=1, source_target_pairs={{0,1},{1,0},{2,3},{3,2},{4,5},{5,4},{6,7},{7,6},{8,9},{9,8},{10,11... | collective-permute-start | bytes 1179656 | tf_op jit(solution)/shard_map/ppermute | solution.py:32
  53.6 3.4 %collective-permute-start.8 = (bf16[256,512]{1,0:T(8,128)(2,1)S(1)}, bf16[256,512]{1,0:T(8,128)(2,1)S(1)}, u32[]{:S(2)}, u32[]{:S(2)}) collective-permute-start(bf16[256,512]{1,0:T(8,128)(2,1)S(1)} %get-tuple-element.17.near_ref), channel_id=1, source_target_pairs={{0,1},{1,0},{2,3},{3,2},{4,5},{5,4},{6,7},{7,6},{8,9},{9,8},{10,11... | collective-permute-start | bytes 786440 | tf_op jit(solution)/shard_map/ppermute | solution.py:32
  55.5 1.5 %copy-start = (bf16[128,4096]{1,0:T(8,128)(2,1)S(1)}, bf16[128,4096]{1,0:T(8,128)(2,1)}, u32[]{:S(2)}) copy-start(bf16[128,4096]{1,0:T(8,128)(2,1)} %out_mine_ref.3) | copy-start | bytes 3145732
  55.5 1.5 %copy-start.1 = (bf16[2,1,48,16,128]{4,3,2,1,0:T(8,128)(2,1)S(1)}, bf16[2,1,48,16,128]{4,3,2,1,0:T(8,128)(2,1)}, u32[]{:S(2)}) copy-start(bf16[2,1,48,16,128]{4,3,2,1,0:T(8,128)(2,1)} %mine_ref.3) | copy-start | bytes 1179652
  58.8 14.8 %collective-permute-start.11 = (bf16[32,4096]{1,0:T(8,128)(2,1)S(1)}, bf16[32,4096]{1,0:T(8,128)(2,1)S(1)}, u32[]{:S(2)}, u32[]{:S(2)}) collective-permute-start(bf16[32,4096]{1,0:T(8,128)(2,1)S(1)} %get-tuple-element.20), channel_id=1, source_target_pairs={{0,6},{1,7},{2,0},{3,1},{4,2},{5,3},{6,4},{7,5},{8,14},{9,15},{10,... | collective-permute-start | bytes 786440 | tf_op jit(solution)/shard_map/ppermute | solution.py:32
  61.5 12.1 %collective-permute-start.12 = (bf16[32,4096]{1,0:T(8,128)(2,1)S(1)}, bf16[32,4096]{1,0:T(8,128)(2,1)S(1)}, u32[]{:S(2)}, u32[]{:S(2)}) collective-permute-start(bf16[32,4096]{1,0:T(8,128)(2,1)S(1)} %get-tuple-element.21), channel_id=1, source_target_pairs={{0,4},{1,5},{2,6},{3,7},{4,0},{5,1},{6,2},{7,3},{8,12},{9,13},{10,... | collective-permute-start | bytes 786440 | tf_op jit(solution)/shard_map/ppermute | solution.py:32
  63.9 14.9 %collective-permute-start.13 = (bf16[32,4096]{1,0:T(8,128)(2,1)S(1)}, bf16[32,4096]{1,0:T(8,128)(2,1)S(1)}, u32[]{:S(2)}, u32[]{:S(2)}) collective-permute-start(bf16[32,4096]{1,0:T(8,128)(2,1)S(1)} %get-tuple-element.22), channel_id=1, source_target_pairs={{0,2},{1,3},{2,4},{3,5},{4,6},{5,7},{6,0},{7,1},{8,10},{9,11},{10,... | collective-permute-start | bytes 786440 | tf_op jit(solution)/shard_map/ppermute | solution.py:32
  68.8 20.4 %all-to-all-start = ((bf16[4,32,4096]{2,1,0:T(8,128)(2,1)}), bf16[4,32,4096]{2,1,0:T(8,128)(2,1)S(1)}, u32[]{:S(2)}, u32[]{:S(2)}) async-start(bf16[4,32,4096]{2,1,0:T(8,128)(2,1)} %attend.2), calls=%async_computation | async-start | bytes 2097152 | tf_op jit(solution)/shard_map/all_to_all | solution.py:37
  78.9 19.4 %collective-permute-start.14 = (bf16[32,4096]{1,0:T(8,128)(2,1)S(1)}, bf16[32,4096]{1,0:T(8,128)(2,1)S(1)}, u32[]{:S(2)}, u32[]{:S(2)}) collective-permute-start(bf16[32,4096]{1,0:T(8,128)(2,1)S(1)} %add_convert_fusion.1), channel_id=1, source_target_pairs={{0,8},{1,9},{2,10},{3,11},{4,12},{5,13},{6,14},{7,15},{8,0},{9,1},... | collective-permute-start | bytes 786440 | tf_op jit(solution)/shard_map/ppermute | solution.py:32

commit v4 on v3

--- a/solution.py
+++ b/solution.py
@@ -22,9 +22,13 @@
     return (y % 2) * 8 + (x % N_X) * 2 + c % 2
 
 
-def moved(value, dy, dx, dc):
+def place_of(x, step):
+    return ((x ^ (step & 1)) + (step & 2)) & 3
+
+
+def moved(value, dy, step, dc):
     pairs = [
-        (tp_of(y, x, c), tp_of(y + dy, x + dx, c + dc))
+        (tp_of(y, x, c), tp_of(y + dy, place_of(x, step), c + dc))
         for y in range(2)
         for x in range(N_X)
         for c in range(2)
@@ -85,7 +89,7 @@
         slot_owner = slot_owner + (slot >= cache_starts[s] * PAGE).astype(jnp.int32)
 
     yy, cc, dx = row & 1, row >> 1, lane >> 5
-    holder = ((y + yy) & 1) * 8 + ((x - dx) & 3) * 2 + ((c + cc) & 1)
+    holder = ((y + yy) & 1) * 8 + place_of(x, dx) * 2 + ((c + cc) & 1)
     token = holder * BLOCK + (lane & (BLOCK - 1))
     token_owner = pick(token, list(range(SEQS)))
     in_prompt = token - pick(token, starts)
@@ -97,7 +101,7 @@
 
     base = [cache_starts[s + 1] * PAGE - starts[s] for s in range(SEQS)]
     for b in range(8):
-        at = ((y + b // 4) & 1) * 8 + ((x - b % 4) & 3) * 2 + c
+        at = ((y + b // 4) & 1) * 8 + place_of(x, b % 4) * 2 + c
         query = at * BLOCK + lax.broadcasted_iota(jnp.int32, (BLOCK, 128), 0)
         owner = pick(query, list(range(SEQS)))
         reach = pick(query, base) + query
@@ -217,7 +221,7 @@
             rows = partial[i * BLOCK : (i + 1) * BLOCK]
             if len(out_refs) == 1:
                 x = my_place()[1]
-                out_refs[0][(x - i) & 3, :, lanes] = rows
+                out_refs[0][place_of(x, i), :, lanes] = rows
             else:
                 out_refs[i][:, lanes] = rows
 
@@ -372,7 +376,7 @@
     kept = attend(0, operands)
     passed_in = [passed[0]]
     for dx in (1, 2, 3):
-        passed_in.append(moved(passed[dx], 0, -dx, 0))
+        passed_in.append(moved(passed[dx], 0, dx, 0))
     kept_in = along_x(kept[0])
     passed_sum = added(passed_in).astype(jnp.bfloat16)
     from_partner = moved(passed_sum, 1, 0, 0)

time: 99.7 us -> 102 us (1.023)
  the two profiles are of different devices: /device:TPU:1 before, /device:TPU:7 now
where the time goes in v4:
time: 102 us
  starting transfers between devices  61.7 us (60%)
  waiting for transfers between devices  26.7 us (26%)
  Pallas kernels  11.1 us (11%)
  other arithmetic  1.04 us (1%)
    ppermute x15, starting transfers between devices, moved(): return lax.ppermute(value, 'tp', pairs)  55.5 us
    ppermute x15, waiting for transfers between devices, moved(): return lax.ppermute(value, 'tp', pairs)  20.4 us
    all_to_all x1, waiting for transfers between devices, along_x(): return lax.all_to_all(value, 'tp', 0, 0, axis_index_groups=groups)  6.34 us
    all_to_all x1, starting transfers between devices, along_x(): return lax.all_to_all(value, 'tp', 0, 0, axis_index_groups=groups)  6.15 us
    pallas_call x2, Pallas kernels, attend(): pl.pallas_call(functools.partial(attend_kernel, half), out_shape=shapes,...  4.53 us
    pallas_call x1, Pallas kernels, project(): pl.pallas_call(project_kernel, out_shape=(jax.ShapeDtypeStruct((256, 4096...  2.52 us
    pallas_call x1, Pallas kernels, layout_tables(): pl.pallas_call(layout_kernel, out_shape=[jax.ShapeDtypeStruct((256, 1280)...  2.08 us
  transfers between devices with their start and end apart: 16, of which 7 were waited for; matrix products, arithmetic and copies ran while one was open for 0% of the time, Pallas kernels for 9%

profile of v4, /device:TPU:7, one launch (start us, length us, event | category | flops | bytes accessed | tf_op | source)
XLA Modules:
  0.0 101.6 jit_solution(13201893553405103563)
XLA Ops:
  0.6 2.6 %collective-permute-start.7 = (bf16[4096,384]{1,0:T(8,128)(2,1)}, bf16[4096,384]{1,0:T(8,128)(2,1)S(1)}, u32[]{:S(2)}, u32[]{:S(2)}) collective-permute-start(bf16[4096,384]{1,0:T(8,128)(2,1)} %refs_6_.1), channel_id=1, source_target_pairs={{0,1},{1,0},{2,3},{3,2},{4,5},{5,4},{6,7},{7,6},{8,9},{9,8},{10,11... | collective-permute-start | bytes 9437192 | tf_op jit(solution)/shard_map/ppermute | solution.py:36
  3.2 7.5 %collective-permute-start.3 = (bf16[32,4096]{1,0:T(8,128)(2,1)}, bf16[32,4096]{1,0:T(8,128)(2,1)S(1)}, u32[]{:S(2)}, u32[]{:S(2)}) collective-permute-start(bf16[32,4096]{1,0:T(8,128)(2,1)} %refs_5_.1), channel_id=1, source_target_pairs={{0,8},{1,9},{2,10},{3,11},{4,12},{5,13},{6,14},{7,15},{8,0},{9,1},... | collective-permute-start | bytes 786440 | tf_op jit(solution)/shard_map/ppermute | solution.py:36
  10.7 2.2 %collective-permute-start.10 = (bf16[128,4096]{1,0:T(8,128)(2,1)}, bf16[128,4096]{1,0:T(8,128)(2,1)S(1)}, u32[]{:S(2)}, u32[]{:S(2)}) collective-permute-start(bf16[128,4096]{1,0:T(8,128)(2,1)} %out_mine_ref.3), channel_id=1, source_target_pairs={{0,1},{1,0},{2,3},{3,2},{4,5},{5,4},{6,7},{7,6},{8,9},{9,8},{10,11... | collective-permute-start | bytes 3145736 | tf_op jit(solution)/shard_map/ppermute | solution.py:36
  12.9 2.5 %collective-permute-start = (bf16[32,4096]{1,0:T(8,128)(2,1)}, bf16[32,4096]{1,0:T(8,128)(2,1)S(1)}, u32[]{:S(2)}, u32[]{:S(2)}) collective-permute-start(bf16[32,4096]{1,0:T(8,128)(2,1)} %refs_5_.1), channel_id=1, source_target_pairs={{0,2},{1,3},{2,0},{3,1},{4,6},{5,7},{6,4},{7,5},{8,10},{9,11},{10,... | collective-permute-start | bytes 786440 | tf_op jit(solution)/shard_map/ppermute | solution.py:36
  15.4 2.7 %collective-permute-start.1 = (bf16[32,4096]{1,0:T(8,128)(2,1)}, bf16[32,4096]{1,0:T(8,128)(2,1)S(1)}, u32[]{:S(2)}, u32[]{:S(2)}) collective-permute-start(bf16[32,4096]{1,0:T(8,128)(2,1)} %refs_5_.1), channel_id=1, source_target_pairs={{0,4},{1,5},{2,6},{3,7},{4,0},{5,1},{6,2},{7,3},{8,12},{9,13},{10,... | collective-permute-start | bytes 786440 | tf_op jit(solution)/shard_map/ppermute | solution.py:36
  19.1 9.8 %collective-permute-start.2 = (bf16[32,4096]{1,0:T(8,128)(2,1)}, bf16[32,4096]{1,0:T(8,128)(2,1)S(1)}, u32[]{:S(2)}, u32[]{:S(2)}) collective-permute-start(bf16[32,4096]{1,0:T(8,128)(2,1)} %refs_5_.1), channel_id=1, source_target_pairs={{0,6},{1,7},{2,4},{3,5},{4,2},{5,3},{6,0},{7,1},{8,14},{9,15},{10,... | collective-permute-start | bytes 786440 | tf_op jit(solution)/shard_map/ppermute | solution.py:36
  28.9 1.9 %collective-permute-start.4 = (bf16[32,4096]{1,0:T(8,128)(2,1)S(1)}, bf16[32,4096]{1,0:T(8,128)(2,1)S(1)}, u32[]{:S(2)}, u32[]{:S(2)}) collective-permute-start(bf16[32,4096]{1,0:T(8,128)(2,1)S(1)} %collective-permute-done.3.refs_4_), channel_id=1, source_target_pairs={{0,2},{1,3},{2,0},{3,1},{4,6},{5,7},{6,4},{7,5},{8,10},{9,11},{10,... | collective-permute-start | bytes 786440 | tf_op jit(solution)/shard_map/ppermute | solution.py:36
  30.9 3.1 %collective-permute-start.5 = (bf16[32,4096]{1,0:T(8,128)(2,1)S(1)}, bf16[32,4096]{1,0:T(8,128)(2,1)S(1)}, u32[]{:S(2)}, u32[]{:S(2)}) collective-permute-start(bf16[32,4096]{1,0:T(8,128)(2,1)S(1)} %collective-permute-done.3.refs_4_), channel_id=1, source_target_pairs={{0,4},{1,5},{2,6},{3,7},{4,0},{5,1},{6,2},{7,3},{8,12},{9,13},{10,... | collective-permute-start | bytes 786440 | tf_op jit(solution)/shard_map/ppermute | solution.py:36
  35.4 4.3 %collective-permute-start.6 = (bf16[32,4096]{1,0:T(8,128)(2,1)S(1)}, bf16[32,4096]{1,0:T(8,128)(2,1)S(1)}, u32[]{:S(2)}, u32[]{:S(2)}) collective-permute-start(bf16[32,4096]{1,0:T(8,128)(2,1)S(1)} %collective-permute-done.3.refs_4_), channel_id=1, source_target_pairs={{0,6},{1,7},{2,4},{3,5},{4,2},{5,3},{6,0},{7,1},{8,14},{9,15},{10,... | collective-permute-start | bytes 786440 | tf_op jit(solution)/shard_map/ppermute | solution.py:36
  39.7 3.5 %collective-permute-start.9 = (bf16[2,1,48,16,128]{4,3,2,1,0:T(8,128)(2,1)}, bf16[2,1,48,16,128]{4,3,2,1,0:T(8,128)(2,1)S(1)}, u32[]{:S(2)}, u32[]{:S(2)}) collective-permute-start(bf16[2,1,48,16,128]{4,3,2,1,0:T(8,128)(2,1)} %mine_ref.3), channel_id=1, source_target_pairs={{0,1},{1,0},{2,3},{3,2},{4,5},{5,4},{6,7},{7,6},{8,9},{9,8},{10,11... | collective-permute-start | bytes 1179656 | tf_op jit(solution)/shard_map/ppermute | solution.py:36
  43.2 2.1 %layout.1 = (f32[256,1280]{1,0:T(8,128)S(1)}, s32[8,128]{1,0:T(8,128)S(1)}, bf16[32,128]{1,0:T(8,128)(2,1)S(1)}, bf16[32,4096]{1,0:T(8,128)(2,1)S(1)}, bf16[4096,384]{1,0:T(8,128)(2,1)S(1)}) custom-call(s32[4,128]{1,0:T(4,128)} %bitcast.7, s32[8]{0:T(128)} %refs_1_.1, s32[48]{0:T(128)} %refs_2_.1, s32[40]{0:T(128)} %refs_3_.1, bf16[32,128]{1,0:T(8,128)(2,1)} %bitcast.6, ...), custom_call_target="tpu_custom_call" | custom-call | bytes 6000000 | tf_op jit(solution)/shard_map/layout/pallas_call | solution.py:136
  45.3 4.8 %collective-permute-done.6.refs_7_ = bf16[32,4096]{1,0:T(8,128)(2,1)S(1)} collective-permute-done((bf16[32,4096]{1,0:T(8,128)(2,1)S(1)}, bf16[32,4096]{1,0:T(8,128)(2,1)S(1)}, u32[]{:S(2)}, u32[]{:S(2)}) %collective-permute-start.6) | collective-permute-done | bytes 262176 | tf_op jit(solution)/shard_map/ppermute | solution.py:36
  50.0 2.5 %project.1 = (bf16[256,4096]{1,0:T(8,128)(2,1)S(1)}, bf16[256,512]{1,0:T(8,128)(2,1)S(1)}) custom-call(bf16[32,4096]{1,0:T(8,128)(2,1)S(1)} %get-tuple-element.13.refs_0_, bf16[32,4096]{1,0:T(8,128)(2,1)S(1)} %collective-permute-done.refs_1_, bf16[32,4096]{1,0:T(8,128)(2,1)S(1)} %collective-permute-done.1.refs_2_, ...), custom_call_target="tpu_custom_call" | custom-call | flops 1073741824 | bytes 9000000 | tf_op jit(solution)/shard_map/project/pallas_call | solution.py:182
  52.6 2.4 %collective-permute-start.8 = (bf16[256,512]{1,0:T(8,128)(2,1)S(1)}, bf16[256,512]{1,0:T(8,128)(2,1)S(1)}, u32[]{:S(2)}, u32[]{:S(2)}) collective-permute-start(bf16[256,512]{1,0:T(8,128)(2,1)S(1)} %get-tuple-element.17.near_ref), channel_id=1, source_target_pairs={{0,1},{1,0},{2,3},{3,2},{4,5},{5,4},{6,7},{7,6},{8,9},{9,8},{10,11... | collective-permute-start | bytes 786440 | tf_op jit(solution)/shard_map/ppermute | solution.py:36
  56.3 1.8 %attend.3 = (bf16[32,4096]{1,0:T(8,128)(2,1)S(1)}, bf16[32,4096]{1,0:T(8,128)(2,1)S(1)}, bf16[32,4096]{1,0:T(8,128)(2,1)S(1)}, bf16[32,4096]{1,0:T(8,128)(2,1)S(1)}) custom-call(bf16[256,256]{1,0:T(8,128)(2,1)S(1)} %query.1.q_ref, bf16[256,512]{1,0:T(8,128)(2,1)S(1)} %get-tuple-element.17.near_ref, bf16[2,1,48,16,128]{4,3,2,1,0:T(8,128)(2,1)S(1)} %copy-done.1, ...), custom_call_target="tpu_custom_call" | custom-call | flops 436207616 | bytes 6000000 | tf_op jit(solution)/shard_map/attend/pallas_call | solution.py:292
  58.1 1.9 %collective-permute-start.11 = (bf16[32,4096]{1,0:T(8,128)(2,1)S(1)}, bf16[32,4096]{1,0:T(8,128)(2,1)S(1)}, u32[]{:S(2)}, u32[]{:S(2)}) collective-permute-start(bf16[32,4096]{1,0:T(8,128)(2,1)S(1)} %get-tuple-element.20), channel_id=1, source_target_pairs={{0,2},{1,3},{2,0},{3,1},{4,6},{5,7},{6,4},{7,5},{8,10},{9,11},{10,... | collective-permute-start | bytes 786440 | tf_op jit(solution)/shard_map/ppermute | solution.py:36
  60.0 5.7 %collective-permute-start.12 = (bf16[32,4096]{1,0:T(8,128)(2,1)S(1)}, bf16[32,4096]{1,0:T(8,128)(2,1)S(1)}, u32[]{:S(2)}, u32[]{:S(2)}) collective-permute-start(bf16[32,4096]{1,0:T(8,128)(2,1)S(1)} %get-tuple-element.21), channel_id=1, source_target_pairs={{0,4},{1,5},{2,6},{3,7},{4,0},{5,1},{6,2},{7,3},{8,12},{9,13},{10,... | collective-permute-start | bytes 786440 | tf_op jit(solution)/shard_map/ppermute | solution.py:36
  65.7 1.9 %collective-permute-start.13 = (bf16[32,4096]{1,0:T(8,128)(2,1)S(1)}, bf16[32,4096]{1,0:T(8,128)(2,1)S(1)}, u32[]{:S(2)}, u32[]{:S(2)}) collective-permute-start(bf16[32,4096]{1,0:T(8,128)(2,1)S(1)} %get-tuple-element.22), channel_id=1, source_target_pairs={{0,6},{1,7},{2,4},{3,5},{4,2},{5,3},{6,0},{7,1},{8,14},{9,15},{10,... | collective-permute-start | bytes 786440 | tf_op jit(solution)/shard_map/ppermute | solution.py:36
  67.7 2.8 %attend.2 = bf16[4,32,4096]{2,1,0:T(8,128)(2,1)} custom-call(bf16[256,256]{1,0:T(8,128)(2,1)S(1)} %query.1.q_ref, bf16[256,512]{1,0:T(8,128)(2,1)S(1)} %get-tuple-element.17.near_ref, bf16[2,1,48,16,128]{4,3,2,1,0:T(8,128)(2,1)S(1)} %copy-done.1, f32[256,1280]{1,0:T(8,128)S(1)} %get-tuple-element.18.dist_ref, ...), custom_call_target="tpu_custom_call" | custom-call | flops 436207616 | bytes 6000000 | tf_op jit(solution)/shard_map/attend/pallas_call | solution.py:292
  70.4 6.2 %all-to-all-start = ((bf16[4,32,4096]{2,1,0:T(8,128)(2,1)}), bf16[4,32,4096]{2,1,0:T(8,128)(2,1)S(1)}, u32[]{:S(2)}, u32[]{:S(2)}) async-start(bf16[4,32,4096]{2,1,0:T(8,128)(2,1)} %attend.2), calls=%async_computation | async-start | bytes 2097152 | tf_op jit(solution)/shard_map/all_to_all | solution.py:41
  76.6 5.2 %collective-permute-done.13 = bf16[32,4096]{1,0:T(8,128)(2,1)S(1)} collective-permute-done((bf16[32,4096]{1,0:T(8,128)(2,1)S(1)}, bf16[32,4096]{1,0:T(8,128)(2,1)S(1)}, u32[]{:S(2)}, u32[]{:S(2)}) %collective-permute-start.13) | collective-permute-done | bytes 262176 | tf_op jit(solution)/shard_map/ppermute | solution.py:36
  81.9 3.5 %collective-permute-start.14 = (bf16[32,4096]{1,0:T(8,128)(2,1)S(1)}, bf16[32,4096]{1,0:T(8,128)(2,1)S(1)}, u32[]{:S(2)}, u32[]{:S(2)}) collective-permute-start(bf16[32,4096]{1,0:T(8,128)(2,1)S(1)} %add_convert_fusion.1), channel_id=1, source_target_pairs={{0,8},{1,9},{2,10},{3,11},{4,12},{5,13},{6,14},{7,15},{8,0},{9,1},... | collective-permute-start | bytes 786440 | tf_op jit(solution)/shard_map/ppermute | solution.py:36
  86.7 6.3 %all-to-all-done = bf16[4,32,4096]{2,1,0:T(8,128)(2,1)S(1)} async-done(((bf16[4,32,4096]{2,1,0:T(8,128)(2,1)}), bf16[4,32,4096]{2,1,0:T(8,128)(2,1)S(1)}, u32[]{:S(2)}, u32[]{:S(2)}) %all-to-all-start) | async-done | bytes 1048608 | tf_op jit(solution)/shard_map/all_to_all | solution.py:41
  93.2 7.6 %collective-permute-done.14 = bf16[32,4096]{1,0:T(8,128)(2,1)S(1)} collective-permute-done((bf16[32,4096]{1,0:T(8,128)(2,1)S(1)}, bf16[32,4096]{1,0:T(8,128)(2,1)S(1)}, u32[]{:S(2)}, u32[]{:S(2)}) %collective-permute-start.14) | collective-permute-done | bytes 262176 | tf_op jit(solution)/shard_map/ppermute | solution.py:36
  (21 shorter events, 6.0 us)
Async XLA Ops:
  0.6 49.4 %collective-permute-start.7 = (bf16[4096,384]{1,0:T(8,128)(2,1)}, bf16[4096,384]{1,0:T(8,128)(2,1)S(1)}, u32[]{:S(2)}, u32[]{:S(2)}) collective-permute-start(bf16[4096,384]{1,0:T(8,128)(2,1)} %refs_6_.1), channel_id=1, source_target_pairs={{0,1},{1,0},{2,3},{3,2},{4,5},{5,4},{6,7},{7,6},{8,9},{9,8},{10,11... | collective-permute-start | bytes 9437192 | tf_op jit(solution)/shard_map/ppermute | solution.py:36
  3.2 15.9 %collective-permute-start.3 = (bf16[32,4096]{1,0:T(8,128)(2,1)}, bf16[32,4096]{1,0:T(8,128)(2,1)S(1)}, u32[]{:S(2)}, u32[]{:S(2)}) collective-permute-start(bf16[32,4096]{1,0:T(8,128)(2,1)} %refs_5_.1), channel_id=1, source_target_pairs={{0,8},{1,9},{2,10},{3,11},{4,12},{5,13},{6,14},{7,15},{8,0},{9,1},... | collective-permute-start | bytes 786440 | tf_op jit(solution)/shard_map/ppermute | solution.py:36
  10.7 45.1 %collective-permute-start.10 = (bf16[128,4096]{1,0:T(8,128)(2,1)}, bf16[128,4096]{1,0:T(8,128)(2,1)S(1)}, u32[]{:S(2)}, u32[]{:S(2)}) collective-permute-start(bf16[128,4096]{1,0:T(8,128)(2,1)} %out_mine_ref.3), channel_id=1, source_target_pairs={{0,1},{1,0},{2,3},{3,2},{4,5},{5,4},{6,7},{7,6},{8,9},{9,8},{10,11... | collective-permute-start | bytes 3145736 | tf_op jit(solution)/shard_map/ppermute | solution.py:36
  12.9 16.0 %collective-permute-start = (bf16[32,4096]{1,0:T(8,128)(2,1)}, bf16[32,4096]{1,0:T(8,128)(2,1)S(1)}, u32[]{:S(2)}, u32[]{:S(2)}) collective-permute-start(bf16[32,4096]{1,0:T(8,128)(2,1)} %refs_5_.1), channel_id=1, source_target_pairs={{0,2},{1,3},{2,0},{3,1},{4,6},{5,7},{6,4},{7,5},{8,10},{9,11},{10,... | collective-permute-start | bytes 786440 | tf_op jit(solution)/shard_map/ppermute | solution.py:36
  15.4 15.5 %collective-permute-start.1 = (bf16[32,4096]{1,0:T(8,128)(2,1)}, bf16[32,4096]{1,0:T(8,128)(2,1)S(1)}, u32[]{:S(2)}, u32[]{:S(2)}) collective-permute-start(bf16[32,4096]{1,0:T(8,128)(2,1)} %refs_5_.1), channel_id=1, source_target_pairs={{0,4},{1,5},{2,6},{3,7},{4,0},{5,1},{6,2},{7,3},{8,12},{9,13},{10,... | collective-permute-start | bytes 786440 | tf_op jit(solution)/shard_map/ppermute | solution.py:36
  19.1 16.2 %collective-permute-start.2 = (bf16[32,4096]{1,0:T(8,128)(2,1)}, bf16[32,4096]{1,0:T(8,128)(2,1)S(1)}, u32[]{:S(2)}, u32[]{:S(2)}) collective-permute-start(bf16[32,4096]{1,0:T(8,128)(2,1)} %refs_5_.1), channel_id=1, source_target_pairs={{0,6},{1,7},{2,4},{3,5},{4,2},{5,3},{6,0},{7,1},{8,14},{9,15},{10,... | collective-permute-start | bytes 786440 | tf_op jit(solution)/shard_map/ppermute | solution.py:36
  28.9 10.7 %collective-permute-start.4 = (bf16[32,4096]{1,0:T(8,128)(2,1)S(1)}, bf16[32,4096]{1,0:T(8,128)(2,1)S(1)}, u32[]{:S(2)}, u32[]{:S(2)}) collective-permute-start(bf16[32,4096]{1,0:T(8,128)(2,1)S(1)} %collective-permute-done.3.refs_4_), channel_id=1, source_target_pairs={{0,2},{1,3},{2,0},{3,1},{4,6},{5,7},{6,4},{7,5},{8,10},{9,11},{10,... | collective-permute-start | bytes 786440 | tf_op jit(solution)/shard_map/ppermute | solution.py:36
  30.9 14.4 %collective-permute-start.5 = (bf16[32,4096]{1,0:T(8,128)(2,1)S(1)}, bf16[32,4096]{1,0:T(8,128)(2,1)S(1)}, u32[]{:S(2)}, u32[]{:S(2)}) collective-permute-start(bf16[32,4096]{1,0:T(8,128)(2,1)S(1)} %collective-permute-done.3.refs_4_), channel_id=1, source_target_pairs={{0,4},{1,5},{2,6},{3,7},{4,0},{5,1},{6,2},{7,3},{8,12},{9,13},{10,... | collective-permute-start | bytes 786440 | tf_op jit(solution)/shard_map/ppermute | solution.py:36
  35.4 14.7 %collective-permute-start.6 = (bf16[32,4096]{1,0:T(8,128)(2,1)S(1)}, bf16[32,4096]{1,0:T(8,128)(2,1)S(1)}, u32[]{:S(2)}, u32[]{:S(2)}) collective-permute-start(bf16[32,4096]{1,0:T(8,128)(2,1)S(1)} %collective-permute-done.3.refs_4_), channel_id=1, source_target_pairs={{0,6},{1,7},{2,4},{3,5},{4,2},{5,3},{6,0},{7,1},{8,14},{9,15},{10,... | collective-permute-start | bytes 786440 | tf_op jit(solution)/shard_map/ppermute | solution.py:36
  39.7 16.1 %collective-permute-start.9 = (bf16[2,1,48,16,128]{4,3,2,1,0:T(8,128)(2,1)}, bf16[2,1,48,16,128]{4,3,2,1,0:T(8,128)(2,1)S(1)}, u32[]{:S(2)}, u32[]{:S(2)}) collective-permute-start(bf16[2,1,48,16,128]{4,3,2,1,0:T(8,128)(2,1)} %mine_ref.3), channel_id=1, source_target_pairs={{0,1},{1,0},{2,3},{3,2},{4,5},{5,4},{6,7},{7,6},{8,9},{9,8},{10,11... | collective-permute-start | bytes 1179656 | tf_op jit(solution)/shard_map/ppermute | solution.py:36
  52.6 3.6 %collective-permute-start.8 = (bf16[256,512]{1,0:T(8,128)(2,1)S(1)}, bf16[256,512]{1,0:T(8,128)(2,1)S(1)}, u32[]{:S(2)}, u32[]{:S(2)}) collective-permute-start(bf16[256,512]{1,0:T(8,128)(2,1)S(1)} %get-tuple-element.17.near_ref), channel_id=1, source_target_pairs={{0,1},{1,0},{2,3},{3,2},{4,5},{5,4},{6,7},{7,6},{8,9},{9,8},{10,11... | collective-permute-start | bytes 786440 | tf_op jit(solution)/shard_map/ppermute | solution.py:36
  55.0 1.2 %copy-start = (bf16[128,4096]{1,0:T(8,128)(2,1)S(1)}, bf16[128,4096]{1,0:T(8,128)(2,1)}, u32[]{:S(2)}) copy-start(bf16[128,4096]{1,0:T(8,128)(2,1)} %out_mine_ref.3) | copy-start | bytes 3145732
  55.0 1.3 %copy-start.1 = (bf16[2,1,48,16,128]{4,3,2,1,0:T(8,128)(2,1)S(1)}, bf16[2,1,48,16,128]{4,3,2,1,0:T(8,128)(2,1)}, u32[]{:S(2)}) copy-start(bf16[2,1,48,16,128]{4,3,2,1,0:T(8,128)(2,1)} %mine_ref.3) | copy-start | bytes 1179652
  58.1 18.5 %collective-permute-start.11 = (bf16[32,4096]{1,0:T(8,128)(2,1)S(1)}, bf16[32,4096]{1,0:T(8,128)(2,1)S(1)}, u32[]{:S(2)}, u32[]{:S(2)}) collective-permute-start(bf16[32,4096]{1,0:T(8,128)(2,1)S(1)} %get-tuple-element.20), channel_id=1, source_target_pairs={{0,2},{1,3},{2,0},{3,1},{4,6},{5,7},{6,4},{7,5},{8,10},{9,11},{10,... | collective-permute-start | bytes 786440 | tf_op jit(solution)/shard_map/ppermute | solution.py:36
  60.0 16.6 %collective-permute-start.12 = (bf16[32,4096]{1,0:T(8,128)(2,1)S(1)}, bf16[32,4096]{1,0:T(8,128)(2,1)S(1)}, u32[]{:S(2)}, u32[]{:S(2)}) collective-permute-start(bf16[32,4096]{1,0:T(8,128)(2,1)S(1)} %get-tuple-element.21), channel_id=1, source_target_pairs={{0,4},{1,5},{2,6},{3,7},{4,0},{5,1},{6,2},{7,3},{8,12},{9,13},{10,... | collective-permute-start | bytes 786440 | tf_op jit(solution)/shard_map/ppermute | solution.py:36
  65.7 16.1 %collective-permute-start.13 = (bf16[32,4096]{1,0:T(8,128)(2,1)S(1)}, bf16[32,4096]{1,0:T(8,128)(2,1)S(1)}, u32[]{:S(2)}, u32[]{:S(2)}) collective-permute-start(bf16[32,4096]{1,0:T(8,128)(2,1)S(1)} %get-tuple-element.22), channel_id=1, source_target_pairs={{0,6},{1,7},{2,4},{3,5},{4,2},{5,3},{6,0},{7,1},{8,14},{9,15},{10,... | collective-permute-start | bytes 786440 | tf_op jit(solution)/shard_map/ppermute | solution.py:36
  70.4 22.6 %all-to-all-start = ((bf16[4,32,4096]{2,1,0:T(8,128)(2,1)}), bf16[4,32,4096]{2,1,0:T(8,128)(2,1)S(1)}, u32[]{:S(2)}, u32[]{:S(2)}) async-start(bf16[4,32,4096]{2,1,0:T(8,128)(2,1)} %attend.2), calls=%async_computation | async-start | bytes 2097152 | tf_op jit(solution)/shard_map/all_to_all | solution.py:41
  81.9 18.9 %collective-permute-start.14 = (bf16[32,4096]{1,0:T(8,128)(2,1)S(1)}, bf16[32,4096]{1,0:T(8,128)(2,1)S(1)}, u32[]{:S(2)}, u32[]{:S(2)}) collective-permute-start(bf16[32,4096]{1,0:T(8,128)(2,1)S(1)} %add_convert_fusion.1), channel_id=1, source_target_pairs={{0,8},{1,9},{2,10},{3,11},{4,12},{5,13},{6,14},{7,15},{8,0},{9,1},... | collective-permute-start | bytes 786440 | tf_op jit(solution)/shard_map/ppermute | solution.py:36
